TPU v7x, 512 devices: a whole 4x8x8 slice. The times are simulated.
512 devices in a mesh: lat: 128 (over y, z, core), var: 4 (over x).
Axes of the slice: x: 4, y: 8, z: 8, core: 2. Of those that a mesh axis runs over, the one named last changes fastest.
Arguments:
- control: bfloat16 [4, 128, 64, 3072], P('var', 'lat'), may hold values from -6 to 6
- row_order: int32 [128], replicated, may hold values from 0 to 127, each once
- row_length: int32 [128], replicated, may hold values from 16 to 3072, as said below
- vertical: bfloat16 [4, 64, 64], P('var'), may hold values from -0.75 to 0.75
- amplitude: float32 [4, 768], P('var'), may hold values from 0.3 to 3
- meridional: bfloat16 [4, 128, 128], P('var'), may hold values from -16 to 16
- balance: bfloat16 [4, 64, 64], P('var'), may hold values from -0.75 to 0.75
Outputs:
- increment: bfloat16 [4, 128, 64, 3072], P('var', 'lat')
Inputs may be any that keep to these rules, and one draw needn't show every extreme that they name: `row_length`: each a multiple of 4; the two middle latitude rows have exactly 3072 longitudes and the first and last rows 16.
All inputs are finite; a program needn't handle non-finite values.
Results may differ from a plain program's by a relative error of at most 0.0078.
Values may be sent and summed in bfloat16 or wider, within the bound.
A program may use at most 64 MiB of HBM per device.

v0:
```python
import math

import jax
import jax.numpy as jnp
from jax import lax
from jax.sharding import Mesh
from jax.sharding import PartitionSpec as P

LAT = ("lat_0", "lat_1", "lat_2")


def cut_along(value, dim, peers):
    dims = value.shape
    pieces = value.reshape(*dims[:dim], peers, dims[dim] // peers, *dims[dim + 1 :])
    return jnp.moveaxis(pieces, dim, 0)


def laid_out(pieces, dim):
    pieces = jnp.moveaxis(pieces, 0, dim)
    dims = pieces.shape
    return pieces.reshape(*dims[:dim], dims[dim] * dims[dim + 1], *dims[dim + 2 :])


def moved_by_axis(pieces, axes, sequence):
    dims = [lax.axis_size(a) for a in axes]
    pieces = pieces.reshape(*dims, *pieces.shape[1:])
    for k in sequence:
        pieces = lax.all_to_all(pieces, axes[k], split_axis=k, concat_axis=k, tiled=True)
    return pieces.reshape(-1, *pieces.shape[len(axes) :])


def two_step_exchange(value, groups, sequence, split_dim, concat_dim):
    peers = lax.axis_size(groups[0]) * lax.axis_size(groups[1])
    pieces = cut_along(value, split_dim, peers)
    return laid_out(moved_by_axis(pieces, groups, sequence), concat_dim)


def from_root(value, axis, root):
    return lax.dynamic_index_in_dim(lax.all_gather(value, axis), root, 0, keepdims=False)


def zonal_basis(lengths, offset, width, waves):
    columns = offset + jnp.arange(width, dtype=jnp.int32)
    wavenum = jnp.arange(waves, dtype=jnp.int32)
    period = lengths[:, None, None]
    phases = columns[None, :, None] * wavenum[None, None, :] % period
    angles = 2.0 * math.pi * phases.astype(jnp.float32) / period.astype(jnp.float32)
    inside = (columns[None, :, None] < period) & (wavenum[None, None, :] <= (period - 1) // 2)
    cosine = jnp.where(inside, jnp.cos(angles), 0.0)
    sines = jnp.where(inside, jnp.sin(angles), 0.0)
    return jnp.concatenate([cosine, sines], axis=2)


def wave_scaling(lengths, waves):
    wavenum = jnp.arange(waves, dtype=jnp.int32)
    factor = jnp.where(wavenum == 0, 1.0, 2.0).astype(jnp.float32)
    factor = jnp.concatenate([factor, factor])
    return factor[None, :] / lengths.astype(jnp.float32)[:, None]


def body(control, row_order, row_length, vertical, amplitude, meridional, balance):
    fields = control[0]
    row_count, level_count, lon_count = fields.shape
    waves = amplitude.shape[1]
    lat_total = row_order.shape[0]
    lat_index = lax.axis_index(LAT)
    own_rows = lax.dynamic_slice_in_dim(row_order, lat_index * row_count, row_count)
    latitude = jnp.arange(lat_total, dtype=jnp.int32)
    lengths = jnp.sum(
        jnp.where(own_rows[:, None] == latitude[None, :], row_length[None, :], 0), axis=1
    )
    levels = jnp.einsum(
        "ml,rlj->rmj", vertical[0], fields, preferred_element_type=jnp.float32
    ).astype(jnp.bfloat16)
    block_width = math.gcd(lon_count, 256)
    block_count = lon_count // block_width
    scaling = wave_scaling(lengths, waves)

    def analyse_block(blk_idx, summed):
        offset = blk_idx * block_width
        segment = lax.dynamic_slice_in_dim(levels, offset, block_width, 2)
        basis_tab = zonal_basis(lengths, offset, block_width, waves)
        analysis_tab = (basis_tab * scaling[:, None, :]).astype(jnp.bfloat16)
        return summed + jnp.einsum(
            "rmj,rjc->rmc", segment, analysis_tab, preferred_element_type=jnp.float32
        )

    summed = lax.fori_loop(
        0, block_count, analyse_block, jnp.zeros((row_count, level_count, 2 * waves), jnp.float32)
    )
    amp_both = jnp.concatenate([amplitude[0], amplitude[0]])
    coeffs = (summed * amp_both[None, None, :]).astype(jnp.bfloat16)
    slot_mat = meridional[0][row_order][:, row_order]
    is_derived = lax.axis_index("var") > 0
    pencil = two_step_exchange(coeffs, (("lat_0", "lat_1"), "lat_2"), (1, 0), 2, 0)
    flattened = pencil.reshape(lat_total, -1)
    product = jnp.dot(slot_mat, flattened, preferred_element_type=jnp.float32).astype(jnp.bfloat16)
    blended = lax.all_to_all(
        product.reshape(pencil.shape), LAT, split_axis=0, concat_axis=2, tiled=True
    )
    stream = from_root(blended, "var", 0)
    lifted = jnp.einsum("ml,rlc->rmc", balance[0], stream, preferred_element_type=jnp.float32)
    balanced = jnp.where(
        is_derived, (blended.astype(jnp.float32) + lifted).astype(jnp.bfloat16), blended
    )

    def synth_block(blk_idx, output):
        offset = blk_idx * block_width
        basis_tab = zonal_basis(lengths, offset, block_width, waves).astype(jnp.bfloat16)
        segment = jnp.einsum(
            "rmc,rjc->rmj", balanced, basis_tab, preferred_element_type=jnp.float32
        ).astype(jnp.bfloat16)
        return lax.dynamic_update_slice_in_dim(output, segment, offset, 2)

    output = lax.fori_loop(0, block_count, synth_block, jnp.zeros_like(fields))
    return output[None]


def solution(mesh):
    torus = Mesh(
        mesh.devices.reshape(8, 8, 2, mesh.shape["var"]), ("lat_0", "lat_1", "lat_2", "var")
    )
    return jax.shard_map(
        body,
        mesh=torus,
        in_specs=(
            P("var", LAT, None, None),
            P(),
            P(),
            P("var", None, None),
            P("var", None),
            P("var", None, None),
            P("var", None, None),
        ),
        out_specs=P("var", LAT, None, None),
        check_vma=False,
    )
```

profile of v0, /device:TPU:7, one launch (start us, length us, event | category | flops | bytes accessed | tf_op | source)
XLA Modules:
  0.0 395.8 jit_solution(12095917761805249480)
XLA Ops:
  6.0 152.6 %while.34 = (s32[]{:T(128)}, f32[1,64,1536]{2,1,0:T(8,128)S(1)}, bf16[1,64,3072]{2,1,0:T(8,128)(2,1)S(1)}, s32[1]{0:T(128)}, s32[1,1,1]{2,1,0:T(1,128)}, /*index...) while((s32[]{:T(128)}, f32[1,64,1536]{2,1,0:T(8,128)S(1)}, ...), condition=%wide.region_2.4_spmd.clone, body=%wide.region_1.3_spmd.clone.sunk | while | flops 54461960 | bytes 3989757 | solution.py:88
  7.7 10.6 %fusion.60 = (f32[256,768]{1,0:T(8,128)S(1)}, f32[256,768]{1,0:T(8,128)S(1)}) fusion(f32[]{:T(128)} %bitcast.131, pred[]{:T(512)} %bitcast.133, s32[]{:T(128)} %bitcast.134, s32[256]{0:T(256)S(1)} %iota_add_fusion.5, pred[768]{0:T(1024)(128)(4,1)S(1)} %iota_compare_fusion.6, pred[256]{0:T(512)(128)(4,1)S(1)} %broadcast_compare_fusion.5), kind=kLoop, calls=%fused_computation.35.clone.1 | loop fusion | flops 2752512 | bytes 1574921 | tf_op jit(solution)/shard_map/while/body/eval_jaxpr/concatenate | solution.py:51
  20.4 10.6 %fusion.60 = (f32[256,768]{1,0:T(8,128)S(1)}, f32[256,768]{1,0:T(8,128)S(1)}) fusion(f32[]{:T(128)} %bitcast.131, pred[]{:T(512)} %bitcast.133, s32[]{:T(128)} %bitcast.134, s32[256]{0:T(256)S(1)} %iota_add_fusion.5, pred[768]{0:T(1024)(128)(4,1)S(1)} %iota_compare_fusion.6, pred[256]{0:T(512)(128)(4,1)S(1)} %broadcast_compare_fusion.5), kind=kLoop, calls=%fused_computation.35.clone.1 | loop fusion | flops 2752512 | bytes 1574921 | tf_op jit(solution)/shard_map/while/body/eval_jaxpr/concatenate | solution.py:51
  33.1 10.6 %fusion.60 = (f32[256,768]{1,0:T(8,128)S(1)}, f32[256,768]{1,0:T(8,128)S(1)}) fusion(f32[]{:T(128)} %bitcast.131, pred[]{:T(512)} %bitcast.133, s32[]{:T(128)} %bitcast.134, s32[256]{0:T(256)S(1)} %iota_add_fusion.5, pred[768]{0:T(1024)(128)(4,1)S(1)} %iota_compare_fusion.6, pred[256]{0:T(512)(128)(4,1)S(1)} %broadcast_compare_fusion.5), kind=kLoop, calls=%fused_computation.35.clone.1 | loop fusion | flops 2752512 | bytes 1574921 | tf_op jit(solution)/shard_map/while/body/eval_jaxpr/concatenate | solution.py:51
  45.8 10.6 %fusion.60 = (f32[256,768]{1,0:T(8,128)S(1)}, f32[256,768]{1,0:T(8,128)S(1)}) fusion(f32[]{:T(128)} %bitcast.131, pred[]{:T(512)} %bitcast.133, s32[]{:T(128)} %bitcast.134, s32[256]{0:T(256)S(1)} %iota_add_fusion.5, pred[768]{0:T(1024)(128)(4,1)S(1)} %iota_compare_fusion.6, pred[256]{0:T(512)(128)(4,1)S(1)} %broadcast_compare_fusion.5), kind=kLoop, calls=%fused_computation.35.clone.1 | loop fusion | flops 2752512 | bytes 1574921 | tf_op jit(solution)/shard_map/while/body/eval_jaxpr/concatenate | solution.py:51
  58.5 10.6 %fusion.60 = (f32[256,768]{1,0:T(8,128)S(1)}, f32[256,768]{1,0:T(8,128)S(1)}) fusion(f32[]{:T(128)} %bitcast.131, pred[]{:T(512)} %bitcast.133, s32[]{:T(128)} %bitcast.134, s32[256]{0:T(256)S(1)} %iota_add_fusion.5, pred[768]{0:T(1024)(128)(4,1)S(1)} %iota_compare_fusion.6, pred[256]{0:T(512)(128)(4,1)S(1)} %broadcast_compare_fusion.5), kind=kLoop, calls=%fused_computation.35.clone.1 | loop fusion | flops 2752512 | bytes 1574921 | tf_op jit(solution)/shard_map/while/body/eval_jaxpr/concatenate | solution.py:51
  71.2 10.6 %fusion.60 = (f32[256,768]{1,0:T(8,128)S(1)}, f32[256,768]{1,0:T(8,128)S(1)}) fusion(f32[]{:T(128)} %bitcast.131, pred[]{:T(512)} %bitcast.133, s32[]{:T(128)} %bitcast.134, s32[256]{0:T(256)S(1)} %iota_add_fusion.5, pred[768]{0:T(1024)(128)(4,1)S(1)} %iota_compare_fusion.6, pred[256]{0:T(512)(128)(4,1)S(1)} %broadcast_compare_fusion.5), kind=kLoop, calls=%fused_computation.35.clone.1 | loop fusion | flops 2752512 | bytes 1574921 | tf_op jit(solution)/shard_map/while/body/eval_jaxpr/concatenate | solution.py:51
  83.9 10.6 %fusion.60 = (f32[256,768]{1,0:T(8,128)S(1)}, f32[256,768]{1,0:T(8,128)S(1)}) fusion(f32[]{:T(128)} %bitcast.131, pred[]{:T(512)} %bitcast.133, s32[]{:T(128)} %bitcast.134, s32[256]{0:T(256)S(1)} %iota_add_fusion.5, pred[768]{0:T(1024)(128)(4,1)S(1)} %iota_compare_fusion.6, pred[256]{0:T(512)(128)(4,1)S(1)} %broadcast_compare_fusion.5), kind=kLoop, calls=%fused_computation.35.clone.1 | loop fusion | flops 2752512 | bytes 1574921 | tf_op jit(solution)/shard_map/while/body/eval_jaxpr/concatenate | solution.py:51
  96.6 10.6 %fusion.60 = (f32[256,768]{1,0:T(8,128)S(1)}, f32[256,768]{1,0:T(8,128)S(1)}) fusion(f32[]{:T(128)} %bitcast.131, pred[]{:T(512)} %bitcast.133, s32[]{:T(128)} %bitcast.134, s32[256]{0:T(256)S(1)} %iota_add_fusion.5, pred[768]{0:T(1024)(128)(4,1)S(1)} %iota_compare_fusion.6, pred[256]{0:T(512)(128)(4,1)S(1)} %broadcast_compare_fusion.5), kind=kLoop, calls=%fused_computation.35.clone.1 | loop fusion | flops 2752512 | bytes 1574921 | tf_op jit(solution)/shard_map/while/body/eval_jaxpr/concatenate | solution.py:51
  109.3 10.6 %fusion.60 = (f32[256,768]{1,0:T(8,128)S(1)}, f32[256,768]{1,0:T(8,128)S(1)}) fusion(f32[]{:T(128)} %bitcast.131, pred[]{:T(512)} %bitcast.133, s32[]{:T(128)} %bitcast.134, s32[256]{0:T(256)S(1)} %iota_add_fusion.5, pred[768]{0:T(1024)(128)(4,1)S(1)} %iota_compare_fusion.6, pred[256]{0:T(512)(128)(4,1)S(1)} %broadcast_compare_fusion.5), kind=kLoop, calls=%fused_computation.35.clone.1 | loop fusion | flops 2752512 | bytes 1574921 | tf_op jit(solution)/shard_map/while/body/eval_jaxpr/concatenate | solution.py:51
  122.0 10.6 %fusion.60 = (f32[256,768]{1,0:T(8,128)S(1)}, f32[256,768]{1,0:T(8,128)S(1)}) fusion(f32[]{:T(128)} %bitcast.131, pred[]{:T(512)} %bitcast.133, s32[]{:T(128)} %bitcast.134, s32[256]{0:T(256)S(1)} %iota_add_fusion.5, pred[768]{0:T(1024)(128)(4,1)S(1)} %iota_compare_fusion.6, pred[256]{0:T(512)(128)(4,1)S(1)} %broadcast_compare_fusion.5), kind=kLoop, calls=%fused_computation.35.clone.1 | loop fusion | flops 2752512 | bytes 1574921 | tf_op jit(solution)/shard_map/while/body/eval_jaxpr/concatenate | solution.py:51
  134.7 10.6 %fusion.60 = (f32[256,768]{1,0:T(8,128)S(1)}, f32[256,768]{1,0:T(8,128)S(1)}) fusion(f32[]{:T(128)} %bitcast.131, pred[]{:T(512)} %bitcast.133, s32[]{:T(128)} %bitcast.134, s32[256]{0:T(256)S(1)} %iota_add_fusion.5, pred[768]{0:T(1024)(128)(4,1)S(1)} %iota_compare_fusion.6, pred[256]{0:T(512)(128)(4,1)S(1)} %broadcast_compare_fusion.5), kind=kLoop, calls=%fused_computation.35.clone.1 | loop fusion | flops 2752512 | bytes 1574921 | tf_op jit(solution)/shard_map/while/body/eval_jaxpr/concatenate | solution.py:51
  147.4 10.6 %fusion.60 = (f32[256,768]{1,0:T(8,128)S(1)}, f32[256,768]{1,0:T(8,128)S(1)}) fusion(f32[]{:T(128)} %bitcast.131, pred[]{:T(512)} %bitcast.133, s32[]{:T(128)} %bitcast.134, s32[256]{0:T(256)S(1)} %iota_add_fusion.5, pred[768]{0:T(1024)(128)(4,1)S(1)} %iota_compare_fusion.6, pred[256]{0:T(512)(128)(4,1)S(1)} %broadcast_compare_fusion.5), kind=kLoop, calls=%fused_computation.35.clone.1 | loop fusion | flops 2752512 | bytes 1574921 | tf_op jit(solution)/shard_map/while/body/eval_jaxpr/concatenate | solution.py:51
  159.5 4.2 %all_to_all.28 = bf16[2,2,24576]{2,1,0:T(2,128)(2,1)S(1)} all-to-all(bf16[2,2,24576]{2,1,0:T(2,128)(2,1)S(1)} %reshape.450), channel_id=1, replica_groups=mesh['lat_0'=8,'lat_1'=8,'lat_2'=2,'var'=4] {'lat_2'}, dimensions={0} | all-to-all | bytes 393216 | tf_op jit(solution)/shard_map/all_to_all | solution.py:28
  165.4 16.3 %all-to-all-start.1 = ((bf16[64,2,768]{2,1,0:T(2,128)(2,1)}), bf16[64,2,768]{2,1,0:T(2,128)(2,1)S(1)}, u32[]{:S(2)}, u32[]{:S(2)}) async-start(bf16[64,2,768]{2,1,0:T(2,128)(2,1)} %reshape.452), calls=%async_computation.1 | async-start | bytes 393216 | tf_op jit(solution)/shard_map/all_to_all | solution.py:28
  183.3 10.3 %all-to-all-done.1 = bf16[64,2,768]{2,1,0:T(2,128)(2,1)S(1)} async-done(((bf16[64,2,768]{2,1,0:T(2,128)(2,1)}), bf16[64,2,768]{2,1,0:T(2,128)(2,1)S(1)}, u32[]{:S(2)}, u32[]{:S(2)}) %all-to-all-start.1) | async-done | bytes 196640 | tf_op jit(solution)/shard_map/all_to_all | solution.py:28
  202.2 8.0 %all-to-all-start.2 = ((bf16[128,2,384]{2,1,0:T(2,128)(2,1)}), bf16[128,2,384]{2,1,0:T(2,128)(2,1)S(1)}, u32[]{:S(2)}, u32[]{:S(2)}) async-start(bf16[128,2,384]{2,1,0:T(2,128)(2,1)} %reshape.454), calls=%async_computation.2 | async-start | bytes 393216 | tf_op jit(solution)/shard_map/all_to_all | solution.py:98
  210.2 13.3 %all-to-all-done.2 = bf16[128,2,384]{2,1,0:T(2,128)(2,1)S(1)} async-done(((bf16[128,2,384]{2,1,0:T(2,128)(2,1)}), bf16[128,2,384]{2,1,0:T(2,128)(2,1)S(1)}, u32[]{:S(2)}, u32[]{:S(2)}) %all-to-all-start.2) | async-done | bytes 196640 | tf_op jit(solution)/shard_map/all_to_all | solution.py:98
  224.3 10.9 %all_gather.7 = bf16[4,1,64,1536]{3,2,1,0:T(8,128)(2,1)S(1)} all-gather(bf16[1,1,64,1536]{3,2,1,0:T(8,128)(2,1)S(1)} %copy.38), channel_id=1, replica_groups=mesh['lat_0'=8,'lat_1'=8,'lat_2'=2,'var'=4] {'var'}, dimensions={0}, use_global_device_ids=true | all-gather | bytes 983040 | tf_op jit(solution)/shard_map/all_gather | solution.py:39
  235.7 159.4 %while.33 = (s32[]{:T(128)}, bf16[1,64,3072]{2,1,0:T(8,128)(2,1)S(1)}, s32[1]{0:T(128)}, s32[1,1,1]{2,1,0:T(1,128)}, f32[1,1,1]{2,1,0:T(1,128)}, /*index=5*/bf16...) while((s32[]{:T(128)}, ...), condition=%wide.region_4.6_spmd, body=%wide.region_3.5_spmd.sunk | while | flops 55068168 | bytes 1806559 | solution.py:115
  237.6 11.2 %fusion.56 = (bf16[256,768]{1,0:T(8,128)(2,1)S(1)}, bf16[256,768]{1,0:T(8,128)(2,1)S(1)}) fusion(f32[]{:T(128)} %bitcast.122, pred[]{:T(512)} %bitcast.124, s32[]{:T(128)} %bitcast.125, s32[256]{0:T(256)S(1)} %iota_add_fusion.4, pred[768]{0:T(1024)(128)(4,1)S(1)} %iota_compare_fusion.5, pred[256]{0:T(512)(128)(4,1)S(1)} %broadcast_compare_fusion.4), kind=kLoop, calls=%fused_computation.22.clone.1 | loop fusion | flops 3145728 | bytes 788489 | tf_op jit(solution)/shard_map/while/body/eval_jaxpr/concatenate | solution.py:51
  250.9 11.2 %fusion.56 = (bf16[256,768]{1,0:T(8,128)(2,1)S(1)}, bf16[256,768]{1,0:T(8,128)(2,1)S(1)}) fusion(f32[]{:T(128)} %bitcast.122, pred[]{:T(512)} %bitcast.124, s32[]{:T(128)} %bitcast.125, s32[256]{0:T(256)S(1)} %iota_add_fusion.4, pred[768]{0:T(1024)(128)(4,1)S(1)} %iota_compare_fusion.5, pred[256]{0:T(512)(128)(4,1)S(1)} %broadcast_compare_fusion.4), kind=kLoop, calls=%fused_computation.22.clone.1 | loop fusion | flops 3145728 | bytes 788489 | tf_op jit(solution)/shard_map/while/body/eval_jaxpr/concatenate | solution.py:51
  264.1 11.2 %fusion.56 = (bf16[256,768]{1,0:T(8,128)(2,1)S(1)}, bf16[256,768]{1,0:T(8,128)(2,1)S(1)}) fusion(f32[]{:T(128)} %bitcast.122, pred[]{:T(512)} %bitcast.124, s32[]{:T(128)} %bitcast.125, s32[256]{0:T(256)S(1)} %iota_add_fusion.4, pred[768]{0:T(1024)(128)(4,1)S(1)} %iota_compare_fusion.5, pred[256]{0:T(512)(128)(4,1)S(1)} %broadcast_compare_fusion.4), kind=kLoop, calls=%fused_computation.22.clone.1 | loop fusion | flops 3145728 | bytes 788489 | tf_op jit(solution)/shard_map/while/body/eval_jaxpr/concatenate | solution.py:51
  277.4 11.2 %fusion.56 = (bf16[256,768]{1,0:T(8,128)(2,1)S(1)}, bf16[256,768]{1,0:T(8,128)(2,1)S(1)}) fusion(f32[]{:T(128)} %bitcast.122, pred[]{:T(512)} %bitcast.124, s32[]{:T(128)} %bitcast.125, s32[256]{0:T(256)S(1)} %iota_add_fusion.4, pred[768]{0:T(1024)(128)(4,1)S(1)} %iota_compare_fusion.5, pred[256]{0:T(512)(128)(4,1)S(1)} %broadcast_compare_fusion.4), kind=kLoop, calls=%fused_computation.22.clone.1 | loop fusion | flops 3145728 | bytes 788489 | tf_op jit(solution)/shard_map/while/body/eval_jaxpr/concatenate | solution.py:51
  290.7 11.2 %fusion.56 = (bf16[256,768]{1,0:T(8,128)(2,1)S(1)}, bf16[256,768]{1,0:T(8,128)(2,1)S(1)}) fusion(f32[]{:T(128)} %bitcast.122, pred[]{:T(512)} %bitcast.124, s32[]{:T(128)} %bitcast.125, s32[256]{0:T(256)S(1)} %iota_add_fusion.4, pred[768]{0:T(1024)(128)(4,1)S(1)} %iota_compare_fusion.5, pred[256]{0:T(512)(128)(4,1)S(1)} %broadcast_compare_fusion.4), kind=kLoop, calls=%fused_computation.22.clone.1 | loop fusion | flops 3145728 | bytes 788489 | tf_op jit(solution)/shard_map/while/body/eval_jaxpr/concatenate | solution.py:51
  303.9 11.2 %fusion.56 = (bf16[256,768]{1,0:T(8,128)(2,1)S(1)}, bf16[256,768]{1,0:T(8,128)(2,1)S(1)}) fusion(f32[]{:T(128)} %bitcast.122, pred[]{:T(512)} %bitcast.124, s32[]{:T(128)} %bitcast.125, s32[256]{0:T(256)S(1)} %iota_add_fusion.4, pred[768]{0:T(1024)(128)(4,1)S(1)} %iota_compare_fusion.5, pred[256]{0:T(512)(128)(4,1)S(1)} %broadcast_compare_fusion.4), kind=kLoop, calls=%fused_computation.22.clone.1 | loop fusion | flops 3145728 | bytes 788489 | tf_op jit(solution)/shard_map/while/body/eval_jaxpr/concatenate | solution.py:51
  317.2 11.2 %fusion.56 = (bf16[256,768]{1,0:T(8,128)(2,1)S(1)}, bf16[256,768]{1,0:T(8,128)(2,1)S(1)}) fusion(f32[]{:T(128)} %bitcast.122, pred[]{:T(512)} %bitcast.124, s32[]{:T(128)} %bitcast.125, s32[256]{0:T(256)S(1)} %iota_add_fusion.4, pred[768]{0:T(1024)(128)(4,1)S(1)} %iota_compare_fusion.5, pred[256]{0:T(512)(128)(4,1)S(1)} %broadcast_compare_fusion.4), kind=kLoop, calls=%fused_computation.22.clone.1 | loop fusion | flops 3145728 | bytes 788489 | tf_op jit(solution)/shard_map/while/body/eval_jaxpr/concatenate | solution.py:51
  330.4 11.2 %fusion.56 = (bf16[256,768]{1,0:T(8,128)(2,1)S(1)}, bf16[256,768]{1,0:T(8,128)(2,1)S(1)}) fusion(f32[]{:T(128)} %bitcast.122, pred[]{:T(512)} %bitcast.124, s32[]{:T(128)} %bitcast.125, s32[256]{0:T(256)S(1)} %iota_add_fusion.4, pred[768]{0:T(1024)(128)(4,1)S(1)} %iota_compare_fusion.5, pred[256]{0:T(512)(128)(4,1)S(1)} %broadcast_compare_fusion.4), kind=kLoop, calls=%fused_computation.22.clone.1 | loop fusion | flops 3145728 | bytes 788489 | tf_op jit(solution)/shard_map/while/body/eval_jaxpr/concatenate | solution.py:51
  343.7 11.2 %fusion.56 = (bf16[256,768]{1,0:T(8,128)(2,1)S(1)}, bf16[256,768]{1,0:T(8,128)(2,1)S(1)}) fusion(f32[]{:T(128)} %bitcast.122, pred[]{:T(512)} %bitcast.124, s32[]{:T(128)} %bitcast.125, s32[256]{0:T(256)S(1)} %iota_add_fusion.4, pred[768]{0:T(1024)(128)(4,1)S(1)} %iota_compare_fusion.5, pred[256]{0:T(512)(128)(4,1)S(1)} %broadcast_compare_fusion.4), kind=kLoop, calls=%fused_computation.22.clone.1 | loop fusion | flops 3145728 | bytes 788489 | tf_op jit(solution)/shard_map/while/body/eval_jaxpr/concatenate | solution.py:51
  357.0 11.2 %fusion.56 = (bf16[256,768]{1,0:T(8,128)(2,1)S(1)}, bf16[256,768]{1,0:T(8,128)(2,1)S(1)}) fusion(f32[]{:T(128)} %bitcast.122, pred[]{:T(512)} %bitcast.124, s32[]{:T(128)} %bitcast.125, s32[256]{0:T(256)S(1)} %iota_add_fusion.4, pred[768]{0:T(1024)(128)(4,1)S(1)} %iota_compare_fusion.5, pred[256]{0:T(512)(128)(4,1)S(1)} %broadcast_compare_fusion.4), kind=kLoop, calls=%fused_computation.22.clone.1 | loop fusion | flops 3145728 | bytes 788489 | tf_op jit(solution)/shard_map/while/body/eval_jaxpr/concatenate | solution.py:51
  370.2 11.2 %fusion.56 = (bf16[256,768]{1,0:T(8,128)(2,1)S(1)}, bf16[256,768]{1,0:T(8,128)(2,1)S(1)}) fusion(f32[]{:T(128)} %bitcast.122, pred[]{:T(512)} %bitcast.124, s32[]{:T(128)} %bitcast.125, s32[256]{0:T(256)S(1)} %iota_add_fusion.4, pred[768]{0:T(1024)(128)(4,1)S(1)} %iota_compare_fusion.5, pred[256]{0:T(512)(128)(4,1)S(1)} %broadcast_compare_fusion.4), kind=kLoop, calls=%fused_computation.22.clone.1 | loop fusion | flops 3145728 | bytes 788489 | tf_op jit(solution)/shard_map/while/body/eval_jaxpr/concatenate | solution.py:51
  383.5 11.2 %fusion.56 = (bf16[256,768]{1,0:T(8,128)(2,1)S(1)}, bf16[256,768]{1,0:T(8,128)(2,1)S(1)}) fusion(f32[]{:T(128)} %bitcast.122, pred[]{:T(512)} %bitcast.124, s32[]{:T(128)} %bitcast.125, s32[256]{0:T(256)S(1)} %iota_add_fusion.4, pred[768]{0:T(1024)(128)(4,1)S(1)} %iota_compare_fusion.5, pred[256]{0:T(512)(128)(4,1)S(1)} %broadcast_compare_fusion.4), kind=kLoop, calls=%fused_computation.22.clone.1 | loop fusion | flops 3145728 | bytes 788489 | tf_op jit(solution)/shard_map/while/body/eval_jaxpr/concatenate | solution.py:51
  (158 shorter events, 40.6 us)
Async XLA Ops:
  0.0 5.0 %copy-start = (bf16[1,1,64,3072]{3,2,1,0:T(8,128)(2,1)S(1)}, bf16[1,1,64,3072]{3,2,1,0:T(8,128)(2,1)}, u32[]{:S(2)}) copy-start(bf16[1,1,64,3072]{3,2,1,0:T(8,128)(2,1)} %param.13) | copy-start | bytes 1179652
  6.0 152.6 %copy-start.3 = (f32[1,768]{1,0:T(1,128)S(1)}, f32[1,768]{1,0:T(1,128)}, u32[]{:S(2)}) copy-start(f32[1,768]{1,0:T(1,128)} %param.17) | copy-start | bytes 9220
  159.2 22.5 %copy-start.5 = (s32[128]{0:T(128)S(1)}, s32[128]{0:T(128)}, u32[]{:S(2)}) copy-start(s32[128]{0:T(128)} %param.14) | copy-start | bytes 1540
  159.2 22.5 %copy-start.1 = (bf16[1,128,128]{2,1,0:T(8,128)(2,1)S(1)}, bf16[1,128,128]{2,1,0:T(8,128)(2,1)}, u32[]{:S(2)}) copy-start(bf16[1,128,128]{2,1,0:T(8,128)(2,1)} %param.18) | copy-start | bytes 98308
  165.4 28.2 %all-to-all-start.1 = ((bf16[64,2,768]{2,1,0:T(2,128)(2,1)}), bf16[64,2,768]{2,1,0:T(2,128)(2,1)S(1)}, u32[]{:S(2)}, u32[]{:S(2)}) async-start(bf16[64,2,768]{2,1,0:T(2,128)(2,1)} %reshape.452), calls=%async_computation.1 | async-start | bytes 393216 | tf_op jit(solution)/shard_map/all_to_all | solution.py:28
  202.2 21.3 %all-to-all-start.2 = ((bf16[128,2,384]{2,1,0:T(2,128)(2,1)}), bf16[128,2,384]{2,1,0:T(2,128)(2,1)S(1)}, u32[]{:S(2)}, u32[]{:S(2)}) async-start(bf16[128,2,384]{2,1,0:T(2,128)(2,1)} %reshape.454), calls=%async_computation.2 | async-start | bytes 393216 | tf_op jit(solution)/shard_map/all_to_all | solution.py:98
  224.0 11.4 %copy-start.4 = (bf16[1,64,64]{2,1,0:T(8,128)(2,1)S(1)}, bf16[1,64,64]{2,1,0:T(8,128)(2,1)}, u32[]{:S(2)}) copy-start(bf16[1,64,64]{2,1,0:T(8,128)(2,1)} %param.19) | copy-start | bytes 24580
  395.0 0.7 copy-start.2
where the time goes:
time: 401 us; the launch traced here: 396 us
  other arithmetic  277 us (69%)
  loops' own time  28.8 us (7%)
  starting transfers between devices  24.3 us (6%)
  waiting for transfers between devices  23.6 us (6%)
  local copies, waits for them, and re-layouts  15.4 us (4%)
  blocking collectives  15.1 us (4%)
  matrix products  9.12 us (2%)
    concatenate x24, other arithmetic, zonal_basis(): return jnp.concatenate([cosine, sines], axis=2)  261 us
    all_to_all x1, starting transfers between devices, moved_by_axis(): lax.all_to_all(pieces, axes[k], split_axis=k, concat_axis=k, tiled=True)  16.3 us
    another operation x1, loops' own time, body(): lax.fori_loop(0, block_count, analyse_block, jnp.zeros((row_count, level_...  14.5 us
    another operation x1, loops' own time, body(): output = lax.fori_loop(0, block_count, synth_block, jnp.zeros_like(fields))  14.3 us
    lt x24, other arithmetic, zonal_basis(): columns[None, :, None] < period  13.5 us
    all_to_all x1, waiting for transfers between devices, body(): lax.all_to_all(product.reshape(pencil.shape), LAT, split_axis=0, concat_a...  13.3 us
    all_gather x1, blocking collectives, from_root(): lax.all_gather(value, axis)  10.9 us
    all_to_all x1, waiting for transfers between devices, moved_by_axis(): lax.all_to_all(pieces, axes[k], split_axis=k, concat_axis=k, tiled=True)  10.3 us
  transfers between devices with their start and end apart: 2, of which 2 were waited for; matrix products, arithmetic and copies ran while one was open for 0% of the time, Pallas kernels for 0%

commit v1 on v0

v1 whole, which is shorter than its diff:
```python
import functools
import math

import jax
import jax.numpy as jnp
from jax import lax
from jax.experimental import pallas as pl
from jax.experimental.pallas import tpu as pltpu
from jax.sharding import PartitionSpec as P

LANES = 128
SUBS = 8
F32 = jnp.float32
BF16 = jnp.bfloat16
MESH = pl.DeviceIdType.MESH


def iota(shape, dim):
    return lax.broadcasted_iota(jnp.int32, shape, dim)


def nt_dot(a, b):
    return lax.dot_general(a, b, (((1,), (1,)), ((), ())), preferred_element_type=F32)


def own_length(order_ref, length_ref):
    return length_ref[order_ref[lax.axis_index("lat")]]


def wave_seeds(period, cos_ref, sin_ref, groups, per_peer):
    shape = cos_ref.shape
    row = iota(shape, 0)
    local = row - groups
    fine = 4 * (local % SUBS) + local // SUBS
    wave = jnp.where(row < groups, 4 * per_peer * row, fine).astype(F32)
    phase = wave * iota(shape, 1).astype(F32)
    inverse = 1.0 / period
    phase = phase - jnp.floor(phase * inverse + 0.5) * period
    quadrant = jnp.floor(phase * (4.0 * inverse) + 0.5)
    angle = (4.0 * phase - quadrant * period) * inverse * (0.5 * math.pi)
    sq = angle * angle
    sine = angle * (1.0 + sq * (-1.0 / 6 + sq * (1.0 / 120 + sq * (-1.0 / 5040 + sq * (1.0 / 362880)))))
    cosine = 1.0 + sq * (-0.5 + sq * (1.0 / 24 + sq * (-1.0 / 720 + sq * (1.0 / 40320))))
    odd = jnp.abs(quadrant) == 1.0
    flip = jnp.abs(quadrant) == 2.0
    sign = jnp.where(flip, -1.0, jnp.where(odd, quadrant, 1.0))
    cos_ref[...] = jnp.where(odd, -sign * sine, sign * cosine)
    sin_ref[...] = jnp.where(odd, sign * cosine, sign * sine)


def fill_table(cos_ref, sin_ref, table_ref, groups, quarter):
    rows = groups * SUBS
    blocks = quarter // LANES

    def one(step, carry):
        rem = step // blocks
        start = pl.multiple_of(step % blocks * LANES, LANES)
        cols = pl.ds(start, LANES)
        fine = pl.ds(pl.multiple_of(groups + rem * SUBS, SUBS), SUBS)
        cos_c = cos_ref[pl.ds(0, groups), cols][:, None, :]
        sin_c = sin_ref[pl.ds(0, groups), cols][:, None, :]
        cos_f = cos_ref[fine, cols][None, :, :]
        sin_f = sin_ref[fine, cols][None, :, :]
        cosine = cos_c * cos_f - sin_c * sin_f
        sine = sin_c * cos_f + cos_c * sin_f
        dest = pl.ds(pl.multiple_of(rem * rows, rows), rows)
        table_ref[dest, cols] = cosine.reshape(rows, LANES).astype(BF16)
        table_ref[dest, pl.ds(pl.multiple_of(start + quarter, LANES), LANES)] = sine.reshape(
            rows, LANES
        ).astype(BF16)
        return carry

    lax.fori_loop(0, 4 * blocks, one, 0)


def row_wave(lat_total, per_peer):
    groups = lat_total // 4
    shape = (lat_total, SUBS, LANES)
    peer = iota(shape, 0)
    sub = iota(shape, 1)
    wave = 4 * (peer % groups * per_peer + sub) + peer // groups
    return wave, sub < per_peer


def analysis_kernel(
    order_ref, length_ref, control_ref, vertical_ref, coeff_ref, cos_ref, sin_ref, table_ref, level_ref
):
    lat_total, per_peer = coeff_ref.shape[0], coeff_ref.shape[1]
    groups = lat_total // 4
    rows = groups * SUBS
    lons = control_ref.shape[-1]
    quarter = lons // 4
    blocks = quarter // LANES
    length = own_length(order_ref, length_ref)
    period = length.astype(F32)
    wave_seeds(period, cos_ref, sin_ref, groups, per_peer)
    fill_table(cos_ref, sin_ref, table_ref, groups, quarter)
    levels = jnp.dot(vertical_ref[0], control_ref[0, 0], preferred_element_type=F32)
    level_ref[:, pl.ds(0, lons)] = levels.astype(BF16).astype(F32)
    count = levels.shape[0]
    step = length // 4
    lane = iota((count, LANES), 1)

    def shifted(part):
        base = part * step
        start = base // LANES
        shift = base % LANES
        back = (LANES - shift) % LANES
        pieces = []
        rolled = [
            pltpu.roll(
                level_ref[:, pl.ds(pl.multiple_of((start + b) * LANES, LANES), LANES)], back, 1
            )
            for b in range(blocks + 1)
        ]
        for b in range(blocks):
            both = jnp.where(lane < LANES - shift, rolled[b], rolled[b + 1])
            pieces.append(jnp.where(lane + b * LANES < step, both, 0.0))
        return jnp.concatenate(pieces, axis=1)

    x0, x1, x2, x3 = (shifted(q) for q in range(4))
    y0 = ((x0 + x2) + (x1 + x3)).astype(BF16)
    y2 = ((x0 + x2) - (x1 + x3)).astype(BF16)
    a = (x0 - x2).astype(BF16)
    b = (x1 - x3).astype(BF16)
    zero = jnp.zeros_like(y0)
    weights = (
        ((y0, zero), (zero, y0)),
        ((a, -b), (b, a)),
        ((y2, zero), (zero, y2)),
        ((a, b), (-b, a)),
    )
    wave, held = row_wave(lat_total, per_peer)
    scale = jnp.where(wave == 0, 1.0, 2.0) / period
    scale = jnp.where(held & (wave <= (length - 1) // 2), scale, 0.0)
    for rem in range(4):
        upper, lower = weights[rem]
        mixed = jnp.concatenate(
            [jnp.concatenate(upper, axis=1), jnp.concatenate(lower, axis=1)], axis=0
        )
        part = nt_dot(table_ref[pl.ds(rem * rows, rows), :], mixed)
        part = part.reshape(groups, SUBS, LANES) * scale[rem * groups : (rem + 1) * groups]
        coeff_ref[pl.ds(rem * groups, groups)] = part[:, :per_peer, :].astype(BF16)


def synthesis_kernel(
    order_ref, length_ref, balanced_ref, out_ref, cos_ref, sin_ref, table_ref, spec_ref, wide_ref
):
    lat_total, per_peer = balanced_ref.shape[0], balanced_ref.shape[1]
    groups = lat_total // 4
    rows = groups * SUBS
    count, lons = out_ref.shape[-2], out_ref.shape[-1]
    quarter = lons // 4
    blocks = quarter // LANES
    length = own_length(order_ref, length_ref)
    period = length.astype(F32)
    wave_seeds(period, cos_ref, sin_ref, groups, per_peer)
    fill_table(cos_ref, sin_ref, table_ref, groups, quarter)
    wave, _ = row_wave(lat_total, per_peer)
    spec_ref[...] = jnp.zeros_like(spec_ref)
    spec_ref[:, pl.ds(0, per_peer), :] = jnp.where(
        wave[:, :per_peer] <= (length - 1) // 2, balanced_ref[...].astype(F32), 0.0
    )
    turned = spec_ref[...].reshape(lat_total * SUBS, LANES).T.astype(BF16)

    def parts(rem):
        both = turned[:, rem * rows : (rem + 1) * rows]
        return both[:count], both[count:]

    def against(rem, on_cos, on_sin):
        here = pl.ds(rem * rows, rows)
        return jnp.dot(
            on_cos, table_ref[here, pl.ds(0, quarter)], preferred_element_type=F32
        ) + jnp.dot(on_sin, table_ref[here, pl.ds(quarter, quarter)], preferred_element_type=F32)

    c0, s0 = parts(0)
    c1, s1 = parts(1)
    c2, s2 = parts(2)
    c3, s3 = parts(3)
    e0 = against(0, c0, s0)
    e2 = against(2, c2, s2)
    ab = against(
        1, jnp.concatenate([c1, s1], axis=0), jnp.concatenate([s1, -c1], axis=0)
    ) + against(3, jnp.concatenate([c3, -s3], axis=0), jnp.concatenate([s3, c3], axis=0))
    a, b = ab[:count], ab[count:]
    step = length // 4
    lane = iota((count, LANES), 1)
    wide_ref[...] = jnp.zeros_like(wide_ref)
    for part, piece in enumerate(((e0 + e2) + a, (e0 - e2) + b, (e0 + e2) - a, (e0 - e2) - b)):
        base = part * step
        start = base // LANES
        shift = base % LANES
        before = jnp.zeros((count, LANES), F32)
        for blk in range(blocks + 1):
            if blk < blocks:
                own = piece[:, blk * LANES : (blk + 1) * LANES]
                own = jnp.where(lane + blk * LANES < step, own, 0.0)
                rolled = pltpu.roll(own, shift, 1)
            else:
                rolled = jnp.zeros((count, LANES), F32)
            here = pl.ds(pl.multiple_of((start + blk) * LANES, LANES), LANES)
            wide_ref[:, here] += jnp.where(lane >= shift, rolled, before)
            before = rolled
    out_ref[0, 0] = wide_ref[:, pl.ds(0, lons)].astype(BF16)


def blend_kernel(
    order_ref,
    amp_ref,
    coeff_ref,
    meridional_ref,
    balance_ref,
    balanced_ref,
    recv_ref,
    mixed_ref,
    wide_ref,
    root_ref,
    root_out_ref,
    send_sem,
    recv_sem,
    local_sem,
    root_send_sem,
    root_recv_sem,
    back_send_sem,
    back_recv_sem,
):
    lat_total, per_peer = coeff_ref.shape[0], coeff_ref.shape[1]
    groups = lat_total // 4
    me = lax.axis_index("lat")
    var = lax.axis_index("var")
    var_total = lax.axis_size("var")

    def peer_at(step):
        return (me + step * 37) % lat_total

    barrier = pltpu.get_barrier_semaphore()

    def greet(step, carry):
        pl.semaphore_signal(barrier, 1, device_id={"lat": peer_at(step)}, device_id_type=MESH)
        return carry

    lax.fori_loop(1, lat_total, greet, 0)
    for other in range(1, var_total):
        pl.semaphore_signal(
            barrier, 1, device_id={"var": (var + other) % var_total}, device_id_type=MESH
        )
    pick = jnp.where(iota((lat_total, lat_total), 0) == order_ref[...], 1.0, 0.0).astype(BF16)
    slot_mat = jnp.dot(meridional_ref[0], pick, preferred_element_type=F32).astype(BF16)
    slot_mat = lax.dot_general(
        pick, slot_mat, (((0,), (0,)), ((), ())), preferred_element_type=F32
    ).astype(BF16)
    block = balance_ref[0]
    none = jnp.zeros_like(block)
    lift = jnp.concatenate(
        [jnp.concatenate([block, none], axis=1), jnp.concatenate([none, block], axis=1)], axis=0
    )
    pl.semaphore_wait(barrier, lat_total - 1 + var_total - 1)

    def exchange(src_ref, dst_ref, src_sem, dst_sem):
        def send(step, carry):
            peer = peer_at(step)
            pltpu.make_async_remote_copy(
                src_ref=src_ref.at[peer],
                dst_ref=dst_ref.at[me],
                send_sem=src_sem,
                recv_sem=dst_sem,
                device_id={"lat": peer},
                device_id_type=MESH,
            ).start()
            return carry

        lax.fori_loop(1, lat_total, send, 0)
        own = pltpu.make_async_copy(src_ref.at[me], dst_ref.at[me], local_sem)
        own.start()
        own.wait()
        rest = pl.ds(0, lat_total - 1)
        pltpu.make_async_copy(src_ref.at[rest], src_ref.at[rest], src_sem).wait()
        pltpu.make_async_copy(dst_ref.at[rest], dst_ref.at[rest], dst_sem).wait()

    exchange(coeff_ref, recv_ref, send_sem, recv_sem)
    wide_ref[:, pl.ds(0, per_peer), :] = recv_ref[...].astype(F32)
    for sub in range(per_peer):
        row = wide_ref[:, sub, :].astype(BF16)
        wave = 4 * (me % groups * per_peer + sub) + me // groups
        product = jnp.dot(slot_mat, row, preferred_element_type=F32) * amp_ref[0, wave]
        wide_ref[:, sub, :] = product
    blended = wide_ref[...]

    @pl.when(var == 0)
    def _():
        rounded = blended[:, :per_peer, :].astype(BF16)
        mixed_ref[...] = rounded
        root_out_ref[...] = rounded
        copies = []
        for other in (2, 1, 3):
            if other < var_total:
                copies.append(
                    pltpu.make_async_remote_copy(
                        src_ref=root_out_ref,
                        dst_ref=root_ref,
                        send_sem=root_send_sem.at[other],
                        recv_sem=root_recv_sem,
                        device_id={"var": other},
                        device_id_type=MESH,
                    )
                )
        for copy in copies:
            copy.start()
        for copy in copies:
            copy.wait_send()

    @pl.when(var > 0)
    def _():
        pltpu.make_async_copy(root_ref, root_ref, root_recv_sem).wait()
        wide_ref[:, pl.ds(0, per_peer), :] = root_ref[...].astype(F32)
        root = wide_ref[...].reshape(lat_total * SUBS, LANES).astype(BF16)
        lifted = nt_dot(root, lift).reshape(lat_total, SUBS, LANES)
        mixed_ref[...] = (blended + lifted)[:, :per_peer, :].astype(BF16)

    exchange(mixed_ref, balanced_ref, back_send_sem, back_recv_sem)


def body(control, row_order, row_length, vertical, amplitude, meridional, balance):
    lat_total = row_order.shape[0]
    levels, lons = control.shape[2:]
    waves = amplitude.shape[1]
    per_peer = waves // lat_total
    groups = lat_total // 4
    quarter = lons // 4
    vmem = pl.BlockSpec(memory_space=pltpu.VMEM)
    smem = pl.BlockSpec(memory_space=pltpu.SMEM)
    packed = jax.ShapeDtypeStruct((lat_total, per_peer, LANES), BF16)
    seeds = pltpu.VMEM((groups + 4 * SUBS, quarter), F32)
    table = pltpu.VMEM((lat_total * SUBS, 2 * quarter), BF16)
    coeffs = pl.pallas_call(
        analysis_kernel,
        name="analysis",
        out_shape=packed,
        in_specs=[smem, smem, vmem, vmem],
        out_specs=vmem,
        scratch_shapes=[seeds, seeds, table, pltpu.VMEM((levels, lons + LANES), F32)],
    )(row_order, row_length, control, vertical)
    wide = pltpu.VMEM((lat_total, SUBS, LANES), F32)
    block = pltpu.VMEM(packed.shape, BF16)
    dma = pltpu.SemaphoreType.DMA
    balanced = pl.pallas_call(
        blend_kernel,
        name="blend",
        out_shape=packed,
        in_specs=[vmem, smem, vmem, vmem, vmem],
        out_specs=vmem,
        scratch_shapes=[
            block,
            block,
            wide,
            block,
            block,
            dma(()),
            dma(()),
            dma(()),
            dma((4,)),
            dma(()),
            dma(()),
            dma(()),
        ],
        compiler_params=pltpu.CompilerParams(collective_id=0, has_side_effects=True),
    )(row_order.reshape(1, lat_total), amplitude, coeffs, meridional, balance)
    return pl.pallas_call(
        synthesis_kernel,
        name="synthesis",
        out_shape=jax.ShapeDtypeStruct(control.shape, BF16),
        in_specs=[smem, smem, vmem],
        out_specs=vmem,
        scratch_shapes=[seeds, seeds, table, wide, pltpu.VMEM((levels, lons + LANES), F32)],
    )(row_order, row_length, balanced)


def solution(mesh):
    return jax.shard_map(
        body,
        mesh=mesh,
        in_specs=(
            P("var", "lat", None, None),
            P(),
            P(),
            P("var", None, None),
            P("var", None),
            P("var", None, None),
            P("var", None, None),
        ),
        out_specs=P("var", "lat", None, None),
        check_vma=False,
    )
```

time: 401 us -> 65.2 us (0.16)
  the two profiles are of different devices: /device:TPU:7 before, /device:TPU:10 now
where the time goes in v1:
time: 65.2 us; the launch traced here: 65 us
  Pallas kernels  65 us (100%)
    pallas_call x1, Pallas kernels, body(): pl.pallas_call(blend_kernel, name='blend', out_shape=packed, in_specs=[vm...  54.7 us
    pallas_call x1, Pallas kernels, body(): pl.pallas_call(analysis_kernel, name='analysis', out_shape=packed, in_spe...  5.35 us
    pallas_call x1, Pallas kernels, body(): pl.pallas_call(synthesis_kernel, name='synthesis', out_shape=jax.ShapeDty...  4.98 us

profile of v1, /device:TPU:10, one launch (start us, length us, event | category | flops | bytes accessed | tf_op | source)
XLA Modules:
  0.0 65.0 jit_solution(4320710940519270512)
XLA Ops:
  0.0 5.4 %analysis.1.coeff_ref = bf16[128,6,128]{2,1,0:T(8,128)(2,1)} custom-call(s32[128]{0:T(128)} %order_ref.3, s32[128]{0:T(128)} %length_ref.3, bf16[1,1,64,3072]{3,2,1,0:T(8,128)(2,1)} %control_ref.1, bf16[1,64,64]{2,1,0:T(8,128)(2,1)} %vertical_ref.1), custom_call_target="tpu_custom_call" | custom-call | tf_op jit(solution)/shard_map/analysis/pallas_call | solution.py:335
  5.4 54.7 %blend.1.balanced_ref = bf16[128,6,128]{2,1,0:T(8,128)(2,1)} custom-call(s32[1,128]{1,0:T(1,128)} %bitcast.1, f32[1,768]{1,0:T(1,128)} %amp_ref.1, bf16[128,6,128]{2,1,0:T(8,128)(2,1)} %analysis.1.coeff_ref, bf16[1,128,128]{2,1,0:T(8,128)(2,1)} %meridional_ref.1, bf16[1,64,64]{2,1,0:T(8,128)(2,1)} %balance_ref.1), custom_call_target="tpu_custom_call" | custom-call | tf_op jit(solution)/shard_map/blend/pallas_call | solution.py:346
  60.0 5.0 %synthesis.1 = bf16[1,1,64,3072]{3,2,1,0:T(8,128)(2,1)} custom-call(s32[128]{0:T(128)} %order_ref.3, s32[128]{0:T(128)} %length_ref.3, bf16[128,6,128]{2,1,0:T(8,128)(2,1)} %blend.1.balanced_ref), custom_call_target="tpu_custom_call" | custom-call | tf_op jit(solution)/shard_map/synthesis/pallas_call | solution.py:368

commit v2 on v1

v2 whole, which is shorter than its diff:
```python
import functools
import math

import jax
import jax.numpy as jnp
from jax import lax
from jax.experimental import pallas as pl
from jax.experimental.pallas import tpu as pltpu
from jax.sharding import PartitionSpec as P

LANES = 128
SUBS = 8
ROW = 16
F32 = jnp.float32
BF16 = jnp.bfloat16
MESH = pl.DeviceIdType.MESH


def iota(shape, dim):
    return lax.broadcasted_iota(jnp.int32, shape, dim)


def nt_dot(a, b):
    return lax.dot_general(a, b, (((1,), (1,)), ((), ())), preferred_element_type=F32)


def own_length(order_ref, length_ref):
    return length_ref[order_ref[lax.axis_index("lat")]]


def wave_seeds(period, cos_ref, sin_ref, groups, per_peer):
    shape = cos_ref.shape
    row = iota(shape, 0)
    local = row - groups
    fine = 4 * (local % SUBS) + local // SUBS
    wave = jnp.where(row < groups, 4 * per_peer * row, fine).astype(F32)
    phase = wave * iota(shape, 1).astype(F32)
    inverse = 1.0 / period
    phase = phase - jnp.floor(phase * inverse + 0.5) * period
    quadrant = jnp.floor(phase * (4.0 * inverse) + 0.5)
    angle = (4.0 * phase - quadrant * period) * inverse * (0.5 * math.pi)
    sq = angle * angle
    sine = angle * (1.0 + sq * (-1.0 / 6 + sq * (1.0 / 120 + sq * (-1.0 / 5040 + sq * (1.0 / 362880)))))
    cosine = 1.0 + sq * (-0.5 + sq * (1.0 / 24 + sq * (-1.0 / 720 + sq * (1.0 / 40320))))
    odd = jnp.abs(quadrant) == 1.0
    flip = jnp.abs(quadrant) == 2.0
    sign = jnp.where(flip, -1.0, jnp.where(odd, quadrant, 1.0))
    cos_ref[...] = jnp.where(odd, -sign * sine, sign * cosine)
    sin_ref[...] = jnp.where(odd, sign * cosine, sign * sine)


def fill_table(cos_ref, sin_ref, table_ref, groups):
    blocks = table_ref.shape[0] // 2
    rows = groups * SUBS

    def one(step, carry):
        rem, blk = step // blocks, step % blocks
        cols = pl.ds(pl.multiple_of(blk * LANES, LANES), LANES)
        fine = pl.ds(pl.multiple_of(groups + rem * SUBS, SUBS), SUBS)
        cos_f, sin_f = cos_ref[fine, cols], sin_ref[fine, cols]
        for group in range(0, groups, 2):
            cosine, sine = [], []
            for g in (group, group + 1):
                cos_c, sin_c = cos_ref[pl.ds(g, 1), cols], sin_ref[pl.ds(g, 1), cols]
                cosine.append(cos_c * cos_f - sin_c * sin_f)
                sine.append(sin_c * cos_f + cos_c * sin_f)
            dest = pl.ds(pl.multiple_of(rem * rows + group * SUBS, 2 * SUBS), 2 * SUBS)
            table_ref[blk, dest, :] = jnp.concatenate(cosine, axis=0).astype(BF16)
            table_ref[blk + blocks, dest, :] = jnp.concatenate(sine, axis=0).astype(BF16)
        return carry

    lax.fori_loop(0, 4 * blocks, one, 0)


def table_rows(table_ref, rem, rows, first, last):
    here = pl.ds(rem * rows, rows)
    return jnp.concatenate([table_ref[b, here, :] for b in range(first, last)], axis=1)


def row_wave(lat_total, per_peer):
    groups = lat_total // 4
    shape = (lat_total, SUBS, LANES)
    peer = iota(shape, 0)
    sub = iota(shape, 1)
    wave = 4 * (peer % groups * per_peer + sub) + peer // groups
    return wave, sub < per_peer


def analyse(length, per_peer, control_ref, vertical_ref, coeff_ref, table_ref, level_ref):
    lat_total = coeff_ref.shape[0]
    groups = lat_total // 4
    rows = groups * SUBS
    lons = control_ref.shape[-1]
    quarter = lons // 4
    blocks = quarter // LANES
    period = length.astype(F32)
    levels = jnp.dot(vertical_ref[0], control_ref[0, 0], preferred_element_type=F32)
    level_ref[:, pl.ds(0, lons)] = levels.astype(BF16)
    level_ref[:, pl.ds(lons, LANES)] = jnp.zeros((levels.shape[0], LANES), BF16)
    count = levels.shape[0]
    step = length // 4
    lane = iota((count, LANES), 1)
    columns = [level_ref[:, pl.ds(b * LANES, LANES)] for b in range(4 * blocks + 1)]

    def shifted(part):
        base = part * step
        start, shift = base // LANES, base % LANES
        held = columns
        bit = 1 << max(part * blocks, 1).bit_length() - 1
        while bit and part:
            moved = [held[c + bit] if c + bit < len(held) else held[c] for c in range(len(held))]
            set_here = start // bit % 2 == 1
            held = [jnp.where(set_here, m, h) for m, h in zip(moved, held)]
            held = held[: blocks + bit]
            bit //= 2
        pairs = [jnp.concatenate([held[b], held[b + 1]], axis=1) for b in range(blocks)]
        if part:
            turn = (2 * LANES, LANES)
            place = jnp.where(iota(turn, 0) == iota(turn, 1) + shift, 1.0, 0.0).astype(BF16)
            both = jnp.dot(jnp.concatenate(pairs, axis=0), place, preferred_element_type=F32)
            parts = [both[b * count : (b + 1) * count] for b in range(blocks)]
        else:
            parts = [held[b].astype(F32) for b in range(blocks)]
        return jnp.concatenate(
            [jnp.where(lane + b * LANES < step, parts[b], 0.0) for b in range(blocks)], axis=1
        )

    x0, x1, x2, x3 = (shifted(q) for q in range(4))
    y0 = ((x0 + x2) + (x1 + x3)).astype(BF16)
    y2 = ((x0 + x2) - (x1 + x3)).astype(BF16)
    a = (x0 - x2).astype(BF16)
    b = (x1 - x3).astype(BF16)
    zero = jnp.zeros_like(y0)
    weights = (
        ((y0, zero), (zero, y0)),
        ((a, -b), (b, a)),
        ((y2, zero), (zero, y2)),
        ((a, b), (-b, a)),
    )
    wave, held = row_wave(lat_total, per_peer)
    scale = jnp.where(wave == 0, 1.0, 2.0) / period
    scale = jnp.where(held & (wave <= (length - 1) // 2), scale, 0.0)
    for rem in range(4):
        upper, lower = weights[rem]
        mixed = jnp.concatenate(
            [jnp.concatenate(upper, axis=1), jnp.concatenate(lower, axis=1)], axis=0
        )
        part = nt_dot(table_rows(table_ref, rem, rows, 0, 2 * blocks), mixed)
        part = part.reshape(groups, SUBS, LANES) * scale[rem * groups : (rem + 1) * groups]
        coeff_ref[pl.ds(rem * groups, groups)] = part.astype(BF16)


def synthesis_kernel(
    per_peer, order_ref, length_ref, balanced_ref, table_hbm, out_ref, table_ref, wide_ref, sems
):
    lat_total = balanced_ref.shape[0]
    groups = lat_total // 4
    rows = groups * SUBS
    count, lons = out_ref.shape[-2], out_ref.shape[-1]
    quarter = lons // 4
    blocks = quarter // LANES
    length = own_length(order_ref, length_ref)
    loads = []
    for rem in range(4):
        here = pl.ds(rem * rows, rows)
        loads.append(
            pltpu.make_async_copy(table_hbm.at[:, here], table_ref.at[:, here], sems.at[rem])
        )
        loads[-1].start()
    wide_ref[...] = jnp.zeros_like(wide_ref)
    wave, held = row_wave(lat_total, per_peer)
    spectra = jnp.where(
        held & (wave <= (length - 1) // 2), balanced_ref[...].astype(F32), 0.0
    )
    turned = spectra.reshape(lat_total * SUBS, LANES).T.astype(BF16)

    def parts(rem):
        both = turned[:, rem * rows : (rem + 1) * rows]
        return both[:count], both[count:]

    def against(rem, on_cos, on_sin):
        loads[rem].wait()
        return jnp.dot(
            on_cos, table_rows(table_ref, rem, rows, 0, blocks), preferred_element_type=F32
        ) + jnp.dot(
            on_sin, table_rows(table_ref, rem, rows, blocks, 2 * blocks), preferred_element_type=F32
        )

    c0, s0 = parts(0)
    c1, s1 = parts(1)
    c2, s2 = parts(2)
    c3, s3 = parts(3)
    e0 = against(0, c0, s0)
    e2 = against(2, c2, s2)
    ab = against(
        1, jnp.concatenate([c1, s1], axis=0), jnp.concatenate([s1, -c1], axis=0)
    ) + against(3, jnp.concatenate([c3, -s3], axis=0), jnp.concatenate([s3, c3], axis=0))
    a, b = ab[:count], ab[count:]
    step = length // 4
    lane = iota((count, LANES), 1)
    for part, piece in enumerate(((e0 + e2) + a, (e0 - e2) + b, (e0 + e2) - a, (e0 - e2) - b)):
        base = part * step
        start = base // LANES
        shift = base % LANES
        before = jnp.zeros((count, LANES), F32)
        for blk in range(blocks + 1):
            if blk < blocks:
                own = piece[:, blk * LANES : (blk + 1) * LANES]
                own = jnp.where(lane + blk * LANES < step, own, 0.0)
                rolled = pltpu.roll(own, shift, 1)
            else:
                rolled = jnp.zeros((count, LANES), F32)
            here = pl.ds(pl.multiple_of((start + blk) * LANES, LANES), LANES)
            wide_ref[:, here] += jnp.where(lane >= shift, rolled, before)
            before = rolled
    out_ref[0, 0] = wide_ref[:, pl.ds(0, lons)].astype(BF16)


def blend_kernel(
    per_peer,
    order_smem,
    length_ref,
    amp_ref,
    order_ref,
    control_ref,
    vertical_ref,
    meridional_ref,
    balance_ref,
    balanced_ref,
    table_hbm,
    cos_ref,
    sin_ref,
    table_ref,
    level_ref,
    coeff_ref,
    recv_ref,
    wide_ref,
    product_ref,
    root_ref,
    mixed_ref,
    line_sem,
    table_sem,
    local_sem,
    send_sem,
    recv_sem,
    root_send_sem,
    root_recv_sem,
    back_send_sem,
    back_recv_sem,
):
    lat_total = balanced_ref.shape[0]
    groups = lat_total // 4
    me = lax.axis_index("lat")
    var = lax.axis_index("var")
    var_total = lax.axis_size("var")
    row_size = ROW if lat_total % ROW == 0 else 2
    columns = lat_total // row_size
    chips = row_size // 2
    core, spot, line = me % 2, me // 2 % chips, me // row_size
    barrier = pltpu.get_barrier_semaphore()

    def greet(sem, **where):
        pl.semaphore_signal(sem, 1, device_id=where, device_id_type=MESH)

    def greet_column(sem):
        for step in range(1, columns):
            greet(sem, lat=(line + step) % columns * row_size + me % row_size)

    for step in range(1, row_size):
        greet(barrier, lat=line * row_size + (me + step) % row_size)
    greet_column(barrier)
    for step in range(1, var_total):
        greet(barrier, var=(var + step) % var_total)

    length = own_length(order_smem, length_ref)
    wave_seeds(length.astype(F32), cos_ref, sin_ref, groups, per_peer)
    fill_table(cos_ref, sin_ref, table_ref, groups)
    table_copy = pltpu.make_async_copy(table_ref, table_hbm, table_sem)
    table_copy.start()
    pl.semaphore_wait(barrier, row_size - 1 + columns - 1 + var_total - 1)
    greet_column(line_sem)
    analyse(length, per_peer, control_ref, vertical_ref, coeff_ref, table_ref, level_ref)
    pl.semaphore_wait(line_sem, columns - 1)

    def to_peer(src_ref, dst_ref, peer, src_sem, dst_sem):
        return pltpu.make_async_remote_copy(
            src_ref=src_ref.at[peer],
            dst_ref=dst_ref.at[me],
            send_sem=src_sem,
            recv_sem=dst_sem,
            device_id={"lat": peer},
            device_id_type=MESH,
        )

    def send(step, carry):
        spread = step * 37 % lat_total
        peer = (line + spread // row_size) % columns * row_size
        peer = peer + (spot + spread // 2 % chips) % chips * 2 + (core + spread % 2) % 2
        to_peer(coeff_ref, recv_ref, peer, send_sem, recv_sem).start()
        return carry

    lax.fori_loop(1, lat_total, send, 0)
    own = pltpu.make_async_copy(coeff_ref.at[me], recv_ref.at[me], local_sem)
    own.start()
    pick = jnp.where(iota((lat_total, lat_total), 0) == order_ref[...], 1.0, 0.0).astype(BF16)
    slot_mat = jnp.dot(meridional_ref[0], pick, preferred_element_type=F32).astype(BF16)
    slot_mat = lax.dot_general(
        pick, slot_mat, (((0,), (0,)), ((), ())), preferred_element_type=F32
    ).astype(BF16)
    block = balance_ref[0]
    none = jnp.zeros_like(block)
    lift = jnp.concatenate(
        [jnp.concatenate([block, none], axis=1), jnp.concatenate([none, block], axis=1)], axis=0
    )
    own.wait()
    rest = pl.ds(0, lat_total - 1)

    def settle(ref, sem):
        pltpu.make_async_copy(ref.at[rest], ref.at[rest], sem).wait()

    settle(recv_ref, recv_sem)
    wide_ref[...] = recv_ref[...].astype(F32)
    received = [wide_ref[:, sub, :].astype(BF16) for sub in range(per_peer)]
    product = jnp.dot(slot_mat, jnp.concatenate(received, axis=1), preferred_element_type=F32)
    scaled = []
    for sub in range(per_peer):
        wave = 4 * (me % groups * per_peer + sub) + me // groups
        scaled.append(product[:, sub * LANES : (sub + 1) * LANES] * amp_ref[0, wave])
    product_ref[...] = jnp.concatenate(scaled, axis=1)

    def piece_rows(piece):
        there = (line + columns // 2 - piece + columns) % columns
        return there, pl.ds(pl.multiple_of(there * row_size, row_size), row_size)

    def root_copy(piece, target):
        _, here = piece_rows(piece)
        return pltpu.make_async_remote_copy(
            src_ref=root_ref.at[here],
            dst_ref=root_ref.at[here],
            send_sem=root_send_sem,
            recv_sem=root_recv_sem.at[piece],
            device_id={"var": target},
            device_id_type=MESH,
        )

    half = columns // 2
    relayed = var_total == 4

    @pl.when(var == 0)
    def _():
        root_ref[...] = product_ref[...].astype(BF16)
        for step in range(columns):
            if relayed:
                root_copy(step, 1).start()
                root_copy(columns - 1 - step, 3).start()
            else:
                for target in range(1, var_total):
                    root_copy(step, target).start()

    def one_piece(step, carry):
        outside_in = jnp.where(step % 2 == 0, step // 2, columns - 1 - step // 2)
        piece = jnp.where(var == 1, step, jnp.where(var == 3, columns - 1 - step, outside_in))
        there, here = piece_rows(piece)

        @pl.when(var > 0)
        def _():
            pltpu.make_async_copy(
                root_ref.at[here], root_ref.at[here], root_recv_sem.at[piece]
            ).wait()
            if relayed:

                @pl.when(((var == 1) & (piece < half)) | ((var == 3) & (piece >= half)))
                def _():
                    root_copy(piece, 2).start()

        part = root_ref[here, :]
        stacked = jnp.concatenate(
            [part[:, sub * LANES : (sub + 1) * LANES] for sub in range(per_peer)], axis=0
        )
        lifted = nt_dot(stacked, lift)
        derived = jnp.where(var > 0, 1.0, 0.0)
        for sub in range(per_peer):
            blended = product_ref[here, pl.ds(sub * LANES, LANES)]
            addend = lifted[sub * row_size : (sub + 1) * row_size]
            wide_ref[here, sub, :] = blended + jnp.where(var > 0, addend, 0.0)
        mixed_ref[here] = wide_ref[here].astype(BF16)

        def send_back(offset, inner):
            peer = there * row_size + (me + offset) % row_size

            @pl.when(peer != me)
            def _():
                to_peer(mixed_ref, balanced_ref, peer, back_send_sem, back_recv_sem).start()

            return inner

        lax.fori_loop(0, row_size, send_back, 0)
        return carry

    lax.fori_loop(0, columns, one_piece, 0)
    own = pltpu.make_async_copy(mixed_ref.at[me], balanced_ref.at[me], local_sem)
    own.start()
    own.wait()
    table_copy.wait()
    settle(coeff_ref, send_sem)

    def sent_roots(pieces):
        span = pl.ds(0, pieces * row_size)
        pltpu.make_async_copy(root_ref.at[span], root_ref.at[span], root_send_sem).wait()

    @pl.when(var == 0)
    def _():
        for _ in range(2 if relayed else var_total - 1):
            sent_roots(columns)

    if relayed:

        @pl.when((var == 1) | (var == 3))
        def _():
            sent_roots(half)

    settle(mixed_ref, back_send_sem)
    settle(balanced_ref, back_recv_sem)


def body(control, row_order, row_length, vertical, amplitude, meridional, balance):
    lat_total = row_order.shape[0]
    levels, lons = control.shape[2:]
    waves = amplitude.shape[1]
    per_peer = waves // lat_total
    groups = lat_total // 4
    quarter = lons // 4
    blocks = quarter // LANES
    vmem = pl.BlockSpec(memory_space=pltpu.VMEM)
    smem = pl.BlockSpec(memory_space=pltpu.SMEM)
    anywhere = pl.BlockSpec(memory_space=pl.ANY)
    seeds = pltpu.VMEM((groups + 4 * SUBS, quarter), F32)
    packed = jax.ShapeDtypeStruct((lat_total, SUBS, LANES), BF16)
    table = jax.ShapeDtypeStruct((2 * blocks, lat_total * SUBS, LANES), BF16)
    table_vmem = pltpu.VMEM(table.shape, BF16)
    block = pltpu.VMEM(packed.shape, BF16)
    dma = pltpu.SemaphoreType.DMA
    level = pltpu.VMEM((levels, lons + LANES), F32)
    balanced, basis = pl.pallas_call(
        functools.partial(blend_kernel, per_peer),
        name="blend",
        out_shape=(packed, table),
        in_specs=[smem, smem, smem, vmem, vmem, vmem, vmem, vmem],
        out_specs=(vmem, anywhere),
        scratch_shapes=[
            seeds,
            seeds,
            table_vmem,
            pltpu.VMEM((levels, lons + LANES), BF16),
            block,
            block,
            pltpu.VMEM(packed.shape, F32),
            pltpu.VMEM((lat_total, per_peer * LANES), F32),
            pltpu.VMEM((lat_total, per_peer * LANES), BF16),
            block,
            pltpu.SemaphoreType.REGULAR,
            dma(()),
            dma(()),
            dma(()),
            dma(()),
            dma(()),
            dma((lat_total,)),
            dma(()),
            dma(()),
        ],
        compiler_params=pltpu.CompilerParams(collective_id=0, has_side_effects=True),
    )(
        row_order,
        row_length,
        amplitude,
        row_order.reshape(1, lat_total),
        control,
        vertical,
        meridional,
        balance,
    )
    return pl.pallas_call(
        functools.partial(synthesis_kernel, per_peer),
        name="synthesis",
        out_shape=jax.ShapeDtypeStruct(control.shape, BF16),
        in_specs=[smem, smem, vmem, anywhere],
        out_specs=vmem,
        scratch_shapes=[table_vmem, level, dma((4,))],
    )(row_order, row_length, balanced, basis)


def solution(mesh):
    return jax.shard_map(
        body,
        mesh=mesh,
        in_specs=(
            P("var", "lat", None, None),
            P(),
            P(),
            P("var", None, None),
            P("var", None),
            P("var", None, None),
            P("var", None, None),
        ),
        out_specs=P("var", "lat", None, None),
        check_vma=False,
    )
```

time: 65.2 us -> 50.8 us (0.78)
  the two profiles are of different devices: /device:TPU:10 before, /device:TPU:7 now
where the time goes in v2:
time: 50.8 us; the launch traced here: 50.7 us
  Pallas kernels  50.7 us (100%)
    pallas_call x1, Pallas kernels, body(): pl.pallas_call(functools.partial(blend_kernel, per_peer), name='blend', o...  46.4 us
    pallas_call x1, Pallas kernels, body(): pl.pallas_call(functools.partial(synthesis_kernel, per_peer), name='synth...  4.31 us

profile of v2, /device:TPU:7, one launch (start us, length us, event | category | flops | bytes accessed | tf_op | source)
XLA Modules:
  0.0 50.7 jit_solution(6850217666191053689)
XLA Ops:
  0.0 46.4 %blend.1 = (bf16[128,8,128]{2,1,0:T(8,128)(2,1)}, bf16[12,1024,128]{2,1,0:T(8,128)(2,1)}) custom-call(s32[128]{0:T(128)} %order_ref.1, s32[128]{0:T(128)} %length_ref.3, f32[1,768]{1,0:T(1,128)} %amp_ref.1, s32[1,128]{1,0:T(1,128)} %bitcast.1, bf16[1,1,64,3072]{3,2,1,0:T(8,128)(2,1)} %control_ref.1, bf16[1,64,64]{2,1,0:T(8,128)(2,1)} %vertical_ref.1, ...), custom_call_target="tpu_custom_call" | custom-call | tf_op jit(solution)/shard_map/blend/pallas_call | solution.py:444
  46.4 4.3 %synthesis.1 = bf16[1,1,64,3072]{3,2,1,0:T(8,128)(2,1)} custom-call(s32[128]{0:T(128)} %order_ref.1, s32[128]{0:T(128)} %length_ref.3, bf16[128,8,128]{2,1,0:T(8,128)(2,1)} %get-tuple-element.7.balanced_ref, bf16[12,1024,128]{2,1,0:T(8,128)(2,1)} %get-tuple-element.8.table_hbm), custom_call_target="tpu_custom_call" | custom-call | tf_op jit(solution)/shard_map/synthesis/pallas_call | solution.py:482

commit v3 on v2

--- a/solution.py
+++ b/solution.py
@@ -151,15 +151,34 @@
 
 
 def synthesis_kernel(
-    per_peer, order_ref, length_ref, balanced_ref, table_hbm, out_ref, table_ref, wide_ref, sems
+    per_peer,
+    order_hbm,
+    length_hbm,
+    balanced_hbm,
+    table_hbm,
+    out_hbm,
+    order_ref,
+    length_ref,
+    balanced_ref,
+    out_ref,
+    table_ref,
+    wide_ref,
+    sems,
 ):
     lat_total = balanced_ref.shape[0]
+    arriving = [
+        pltpu.make_async_copy(source, target, sems.at[4 + index])
+        for index, (source, target) in enumerate(
+            ((order_hbm, order_ref), (length_hbm, length_ref), (balanced_hbm, balanced_ref))
+        )
+    ]
+    for copy in arriving:
+        copy.start()
     groups = lat_total // 4
     rows = groups * SUBS
     count, lons = out_ref.shape[-2], out_ref.shape[-1]
     quarter = lons // 4
     blocks = quarter // LANES
-    length = own_length(order_ref, length_ref)
     loads = []
     for rem in range(4):
         here = pl.ds(rem * rows, rows)
@@ -168,6 +187,10 @@
         )
         loads[-1].start()
     wide_ref[...] = jnp.zeros_like(wide_ref)
+    arriving[0].wait()
+    arriving[1].wait()
+    length = own_length(order_ref, length_ref)
+    arriving[2].wait()
     wave, held = row_wave(lat_total, per_peer)
     spectra = jnp.where(
         held & (wave <= (length - 1) // 2), balanced_ref[...].astype(F32), 0.0
@@ -213,11 +236,30 @@
             here = pl.ds(pl.multiple_of((start + blk) * LANES, LANES), LANES)
             wide_ref[:, here] += jnp.where(lane >= shift, rolled, before)
             before = rolled
-    out_ref[0, 0] = wide_ref[:, pl.ds(0, lons)].astype(BF16)
+    leaving = []
+    for part in range(4):
+        here = pl.ds(part * quarter, quarter)
+        out_ref[:, here] = wide_ref[:, here].astype(BF16)
+        leaving.append(
+            pltpu.make_async_copy(out_ref.at[:, here], out_hbm.at[0, 0, :, here], sems.at[7 + part])
+        )
+        leaving[-1].start()
+    for copy in leaving:
+        copy.wait()
 
 
 def blend_kernel(
     per_peer,
+    order_hbm,
+    length_hbm,
+    amp_hbm,
+    order_row_hbm,
+    control_hbm,
+    vertical_hbm,
+    meridional_hbm,
+    balance_hbm,
+    balanced_ref,
+    table_hbm,
     order_smem,
     length_ref,
     amp_ref,
@@ -226,8 +268,7 @@
     vertical_ref,
     meridional_ref,
     balance_ref,
-    balanced_ref,
-    table_hbm,
+    input_sems,
     cos_ref,
     sin_ref,
     table_ref,
@@ -258,6 +299,20 @@
     chips = row_size // 2
     core, spot, line = me % 2, me // 2 % chips, me // row_size
     barrier = pltpu.get_barrier_semaphore()
+    arriving = []
+    for index, (source, target) in enumerate(
+        (
+            (order_hbm, order_smem),
+            (length_hbm, length_ref),
+            (vertical_hbm, vertical_ref),
+            (control_hbm, control_ref),
+            (amp_hbm, amp_ref),
+            (order_row_hbm, order_ref),
+            (meridional_hbm, meridional_ref),
+            (balance_hbm, balance_ref),
+        )
+    ):
+        arriving.append(pltpu.make_async_copy(source, target, input_sems.at[index]))
 
     def greet(sem, **where):
         pl.semaphore_signal(sem, 1, device_id=where, device_id_type=MESH)
@@ -266,12 +321,18 @@
         for step in range(1, columns):
             greet(sem, lat=(line + step) % columns * row_size + me % row_size)
 
+    arriving[0].start()
+    arriving[1].start()
     for step in range(1, row_size):
         greet(barrier, lat=line * row_size + (me + step) % row_size)
     greet_column(barrier)
     for step in range(1, var_total):
         greet(barrier, var=(var + step) % var_total)
-
+    for copy in arriving[2:]:
+        copy.start()
+
+    arriving[0].wait()
+    arriving[1].wait()
     length = own_length(order_smem, length_ref)
     wave_seeds(length.astype(F32), cos_ref, sin_ref, groups, per_peer)
     fill_table(cos_ref, sin_ref, table_ref, groups)
@@ -279,6 +340,8 @@
     table_copy.start()
     pl.semaphore_wait(barrier, row_size - 1 + columns - 1 + var_total - 1)
     greet_column(line_sem)
+    arriving[2].wait()
+    arriving[3].wait()
     analyse(length, per_peer, control_ref, vertical_ref, coeff_ref, table_ref, level_ref)
     pl.semaphore_wait(line_sem, columns - 1)
 
@@ -292,16 +355,30 @@
             device_id_type=MESH,
         )
 
+    def to_line(there, src_ref, dst_ref, src_sem, dst_sem):
+        def one(offset, carry):
+            peer = there * row_size + (me + offset) % row_size
+
+            @pl.when(peer != me)
+            def _():
+                to_peer(src_ref, dst_ref, peer, src_sem, dst_sem).start()
+
+            return carry
+
+        lax.fori_loop(0, row_size, one, 0)
+
     def send(step, carry):
-        spread = step * 37 % lat_total
-        peer = (line + spread // row_size) % columns * row_size
-        peer = peer + (spot + spread // 2 % chips) % chips * 2 + (core + spread % 2) % 2
-        to_peer(coeff_ref, recv_ref, peer, send_sem, recv_sem).start()
+        to_line((line + columns // 2 + step) % columns, coeff_ref, recv_ref, send_sem, recv_sem)
+        to_line((line + columns // 2 - step) % columns, coeff_ref, recv_ref, send_sem, recv_sem)
         return carry
 
-    lax.fori_loop(1, lat_total, send, 0)
+    to_line((line + columns // 2) % columns, coeff_ref, recv_ref, send_sem, recv_sem)
+    lax.fori_loop(1, columns // 2, send, 0)
+    to_line(line, coeff_ref, recv_ref, send_sem, recv_sem)
     own = pltpu.make_async_copy(coeff_ref.at[me], recv_ref.at[me], local_sem)
     own.start()
+    for copy in arriving[4:]:
+        copy.wait()
     pick = jnp.where(iota((lat_total, lat_total), 0) == order_ref[...], 1.0, 0.0).astype(BF16)
     slot_mat = jnp.dot(meridional_ref[0], pick, preferred_element_type=F32).astype(BF16)
     slot_mat = lax.dot_general(
@@ -378,23 +455,13 @@
             [part[:, sub * LANES : (sub + 1) * LANES] for sub in range(per_peer)], axis=0
         )
         lifted = nt_dot(stacked, lift)
-        derived = jnp.where(var > 0, 1.0, 0.0)
         for sub in range(per_peer):
             blended = product_ref[here, pl.ds(sub * LANES, LANES)]
             addend = lifted[sub * row_size : (sub + 1) * row_size]
             wide_ref[here, sub, :] = blended + jnp.where(var > 0, addend, 0.0)
         mixed_ref[here] = wide_ref[here].astype(BF16)
 
-        def send_back(offset, inner):
-            peer = there * row_size + (me + offset) % row_size
-
-            @pl.when(peer != me)
-            def _():
-                to_peer(mixed_ref, balanced_ref, peer, back_send_sem, back_recv_sem).start()
-
-            return inner
-
-        lax.fori_loop(0, row_size, send_back, 0)
+        to_line(there, mixed_ref, balanced_ref, back_send_sem, back_recv_sem)
         return carry
 
     lax.fori_loop(0, columns, one_piece, 0)
@@ -432,7 +499,6 @@
     quarter = lons // 4
     blocks = quarter // LANES
     vmem = pl.BlockSpec(memory_space=pltpu.VMEM)
-    smem = pl.BlockSpec(memory_space=pltpu.SMEM)
     anywhere = pl.BlockSpec(memory_space=pl.ANY)
     seeds = pltpu.VMEM((groups + 4 * SUBS, quarter), F32)
     packed = jax.ShapeDtypeStruct((lat_total, SUBS, LANES), BF16)
@@ -440,14 +506,25 @@
     table_vmem = pltpu.VMEM(table.shape, BF16)
     block = pltpu.VMEM(packed.shape, BF16)
     dma = pltpu.SemaphoreType.DMA
-    level = pltpu.VMEM((levels, lons + LANES), F32)
+    inputs = (
+        pltpu.SMEM(row_order.shape, row_order.dtype),
+        pltpu.SMEM(row_length.shape, row_length.dtype),
+        pltpu.SMEM(amplitude.shape, F32),
+        pltpu.VMEM((1, lat_total), row_order.dtype),
+        pltpu.VMEM(control.shape, BF16),
+        pltpu.VMEM(vertical.shape, BF16),
+        pltpu.VMEM(meridional.shape, BF16),
+        pltpu.VMEM(balance.shape, BF16),
+    )
     balanced, basis = pl.pallas_call(
         functools.partial(blend_kernel, per_peer),
         name="blend",
         out_shape=(packed, table),
-        in_specs=[smem, smem, smem, vmem, vmem, vmem, vmem, vmem],
+        in_specs=[anywhere] * 8,
         out_specs=(vmem, anywhere),
         scratch_shapes=[
+            *inputs,
+            dma((8,)),
             seeds,
             seeds,
             table_vmem,
@@ -483,9 +560,17 @@
         functools.partial(synthesis_kernel, per_peer),
         name="synthesis",
         out_shape=jax.ShapeDtypeStruct(control.shape, BF16),
-        in_specs=[smem, smem, vmem, anywhere],
-        out_specs=vmem,
-        scratch_shapes=[table_vmem, level, dma((4,))],
+        in_specs=[anywhere] * 4,
+        out_specs=anywhere,
+        scratch_shapes=[
+            inputs[0],
+            inputs[1],
+            block,
+            pltpu.VMEM((levels, lons), BF16),
+            table_vmem,
+            pltpu.VMEM((levels, lons + LANES), F32),
+            dma((11,)),
+        ],
     )(row_order, row_length, balanced, basis)
 
 

time: 50.8 us -> 47.1 us (0.927)
  Pallas kernels: 50.7 us -> 46.7 us
    pallas_call x1, Pallas kernels: 46.4 us -> 43.2 us  [body(): pl.pallas_call(functools.partial(blend_kernel, per_peer), name='blend', o...]
    pallas_call x1, Pallas kernels: 4.31 us -> 3.47 us  [body(): pl.pallas_call(functools.partial(synthesis_kernel, per_peer), name='synth...]
where the time goes in v3:
time: 47.1 us; the launch traced here: 46.7 us
  Pallas kernels  46.7 us (99%)
    pallas_call x1, Pallas kernels, body(): pl.pallas_call(functools.partial(blend_kernel, per_peer), name='blend', o...  43.2 us
    pallas_call x1, Pallas kernels, body(): pl.pallas_call(functools.partial(synthesis_kernel, per_peer), name='synth...  3.47 us

profile of v3, /device:TPU:7, one launch (start us, length us, event | category | flops | bytes accessed | tf_op | source)
XLA Modules:
  0.0 46.7 jit_solution(3065315598316449133)
XLA Ops:
  0.0 43.2 %blend.1 = (bf16[128,8,128]{2,1,0:T(8,128)(2,1)}, bf16[12,1024,128]{2,1,0:T(8,128)(2,1)}) custom-call(s32[128]{0:T(128)} %order_hbm.3, s32[128]{0:T(128)} %length_hbm.3, f32[1,768]{1,0:T(1,128)} %amp_hbm.1, s32[1,128]{1,0:T(1,128)} %bitcast.1, bf16[1,1,64,3072]{3,2,1,0:T(8,128)(2,1)} %control_hbm.1, bf16[1,64,64]{2,1,0:T(8,128)(2,1)} %vertical_hbm.1, ...), custom_call_target="tpu_custom_call" | custom-call | tf_op jit(solution)/shard_map/blend/pallas_call | solution.py:519
  43.2 3.5 %synthesis.1 = bf16[1,1,64,3072]{3,2,1,0:T(8,128)(2,1)} custom-call(s32[128]{0:T(128)} %order_hbm.3, s32[128]{0:T(128)} %length_hbm.3, bf16[128,8,128]{2,1,0:T(8,128)(2,1)} %get-tuple-element.7.balanced_hbm, bf16[12,1024,128]{2,1,0:T(8,128)(2,1)} %get-tuple-element.8.table_hbm), custom_call_target="tpu_custom_call" | custom-call | tf_op jit(solution)/shard_map/synthesis/pallas_call | solution.py:559

commit v4 on v3

--- a/solution.py
+++ b/solution.py
@@ -258,7 +258,7 @@
     vertical_hbm,
     meridional_hbm,
     balance_hbm,
-    balanced_ref,
+    balanced_hbm,
     table_hbm,
     order_smem,
     length_ref,
@@ -289,7 +289,7 @@
     back_send_sem,
     back_recv_sem,
 ):
-    lat_total = balanced_ref.shape[0]
+    lat_total = balanced_hbm.shape[0]
     groups = lat_total // 4
     me = lax.axis_index("lat")
     var = lax.axis_index("var")
@@ -317,15 +317,15 @@
     def greet(sem, **where):
         pl.semaphore_signal(sem, 1, device_id=where, device_id_type=MESH)
 
-    def greet_column(sem):
+    def greet_column(sem_of):
         for step in range(1, columns):
-            greet(sem, lat=(line + step) % columns * row_size + me % row_size)
+            greet(sem_of(step), lat=(line + step) % columns * row_size + me % row_size)
 
     arriving[0].start()
     arriving[1].start()
     for step in range(1, row_size):
         greet(barrier, lat=line * row_size + (me + step) % row_size)
-    greet_column(barrier)
+    greet_column(lambda step: barrier)
     for step in range(1, var_total):
         greet(barrier, var=(var + step) % var_total)
     for copy in arriving[2:]:
@@ -339,11 +339,10 @@
     table_copy = pltpu.make_async_copy(table_ref, table_hbm, table_sem)
     table_copy.start()
     pl.semaphore_wait(barrier, row_size - 1 + columns - 1 + var_total - 1)
-    greet_column(line_sem)
+    greet_column(lambda step: line_sem.at[columns - step])
     arriving[2].wait()
     arriving[3].wait()
     analyse(length, per_peer, control_ref, vertical_ref, coeff_ref, table_ref, level_ref)
-    pl.semaphore_wait(line_sem, columns - 1)
 
     def to_peer(src_ref, dst_ref, peer, src_sem, dst_sem):
         return pltpu.make_async_remote_copy(
@@ -355,26 +354,34 @@
             device_id_type=MESH,
         )
 
-    def to_line(there, src_ref, dst_ref, src_sem, dst_sem):
+    def to_line(there, src_ref, dst_ref, src_sem, dst_sem, own=None):
         def one(offset, carry):
             peer = there * row_size + (me + offset) % row_size
 
-            @pl.when(peer != me)
-            def _():
+            def start():
                 to_peer(src_ref, dst_ref, peer, src_sem, dst_sem).start()
 
+            if own is None:
+                pl.when(peer != me)(start)
+            else:
+                start()
             return carry
 
-        lax.fori_loop(0, row_size, one, 0)
+        lax.fori_loop(1 if own else 0, row_size, one, 0, unroll=True)
+
+    def first(distance):
+        pl.semaphore_wait(line_sem.at[distance], 1)
+        there = (line + distance) % columns
+        to_line(there, coeff_ref, recv_ref, send_sem, recv_sem, own=False)
 
     def send(step, carry):
-        to_line((line + columns // 2 + step) % columns, coeff_ref, recv_ref, send_sem, recv_sem)
-        to_line((line + columns // 2 - step) % columns, coeff_ref, recv_ref, send_sem, recv_sem)
+        first(columns // 2 + step)
+        first(columns // 2 - step)
         return carry
 
-    to_line((line + columns // 2) % columns, coeff_ref, recv_ref, send_sem, recv_sem)
+    to_line(line, coeff_ref, recv_ref, send_sem, recv_sem, own=True)
+    first(columns // 2)
     lax.fori_loop(1, columns // 2, send, 0)
-    to_line(line, coeff_ref, recv_ref, send_sem, recv_sem)
     own = pltpu.make_async_copy(coeff_ref.at[me], recv_ref.at[me], local_sem)
     own.start()
     for copy in arriving[4:]:
@@ -406,7 +413,7 @@
     product_ref[...] = jnp.concatenate(scaled, axis=1)
 
     def piece_rows(piece):
-        there = (line + columns // 2 - piece + columns) % columns
+        there = (line + columns // 2 + piece) % columns
         return there, pl.ds(pl.multiple_of(there * row_size, row_size), row_size)
 
     def root_copy(piece, target):
@@ -434,21 +441,34 @@
                 for target in range(1, var_total):
                     root_copy(step, target).start()
 
+    def await_root(piece):
+        _, here = piece_rows(piece)
+        pltpu.make_async_copy(root_ref.at[here], root_ref.at[here], root_recv_sem.at[piece]).wait()
+
+    if relayed:
+        @pl.when((var == 1) | (var == 3))
+        def _():
+            def relay(step, carry):
+                piece = jnp.where(var == 1, step, columns - 1 - step)
+                await_root(piece)
+                root_copy(piece, 2).start()
+                return carry
+
+            lax.fori_loop(0, half, relay, 0)
+
     def one_piece(step, carry):
         outside_in = jnp.where(step % 2 == 0, step // 2, columns - 1 - step // 2)
         piece = jnp.where(var == 1, step, jnp.where(var == 3, columns - 1 - step, outside_in))
         there, here = piece_rows(piece)
 
-        @pl.when(var > 0)
+        waiting = var > 0
+        if relayed:
+            passed_on = ((var == 1) & (piece < half)) | ((var == 3) & (piece >= half))
+            waiting = waiting & jnp.logical_not(passed_on)
+
+        @pl.when(waiting)
         def _():
-            pltpu.make_async_copy(
-                root_ref.at[here], root_ref.at[here], root_recv_sem.at[piece]
-            ).wait()
-            if relayed:
-
-                @pl.when(((var == 1) & (piece < half)) | ((var == 3) & (piece >= half)))
-                def _():
-                    root_copy(piece, 2).start()
+            await_root(piece)
 
         part = root_ref[here, :]
         stacked = jnp.concatenate(
@@ -461,11 +481,11 @@
             wide_ref[here, sub, :] = blended + jnp.where(var > 0, addend, 0.0)
         mixed_ref[here] = wide_ref[here].astype(BF16)
 
-        to_line(there, mixed_ref, balanced_ref, back_send_sem, back_recv_sem)
+        to_line(there, mixed_ref, balanced_hbm, back_send_sem, back_recv_sem)
         return carry
 
     lax.fori_loop(0, columns, one_piece, 0)
-    own = pltpu.make_async_copy(mixed_ref.at[me], balanced_ref.at[me], local_sem)
+    own = pltpu.make_async_copy(mixed_ref.at[me], balanced_hbm.at[me], local_sem)
     own.start()
     own.wait()
     table_copy.wait()
@@ -487,7 +507,7 @@
             sent_roots(half)
 
     settle(mixed_ref, back_send_sem)
-    settle(balanced_ref, back_recv_sem)
+    settle(balanced_hbm, back_recv_sem)
 
 
 def body(control, row_order, row_length, vertical, amplitude, meridional, balance):
@@ -498,7 +518,6 @@
     groups = lat_total // 4
     quarter = lons // 4
     blocks = quarter // LANES
-    vmem = pl.BlockSpec(memory_space=pltpu.VMEM)
     anywhere = pl.BlockSpec(memory_space=pl.ANY)
     seeds = pltpu.VMEM((groups + 4 * SUBS, quarter), F32)
     packed = jax.ShapeDtypeStruct((lat_total, SUBS, LANES), BF16)
@@ -521,7 +540,7 @@
         name="blend",
         out_shape=(packed, table),
         in_specs=[anywhere] * 8,
-        out_specs=(vmem, anywhere),
+        out_specs=(anywhere, anywhere),
         scratch_shapes=[
             *inputs,
             dma((8,)),
@@ -535,7 +554,7 @@
             pltpu.VMEM((lat_total, per_peer * LANES), F32),
             pltpu.VMEM((lat_total, per_peer * LANES), BF16),
             block,
-            pltpu.SemaphoreType.REGULAR,
+            pltpu.SemaphoreType.REGULAR((lat_total,)),
             dma(()),
             dma(()),
             dma(()),

time: 47.1 us -> 47.7 us (1.013)
  Pallas kernels: 46.7 us -> 47.2 us
    pallas_call x1, Pallas kernels: 43.2 us -> 43.8 us  [body(): pl.pallas_call(functools.partial(blend_kernel, per_peer), name='blend', o...]
where the time goes in v4:
time: 47.7 us; the launch traced here: 47.2 us
  Pallas kernels  47.2 us (99%)
    pallas_call x1, Pallas kernels, body(): pl.pallas_call(functools.partial(blend_kernel, per_peer), name='blend', o...  43.8 us
    pallas_call x1, Pallas kernels, body(): pl.pallas_call(functools.partial(synthesis_kernel, per_peer), name='synth...  3.46 us

profile of v4, /device:TPU:7, one launch (start us, length us, event | category | flops | bytes accessed | tf_op | source)
XLA Modules:
  0.0 47.2 jit_solution(5768213004041172432)
XLA Ops:
  0.0 43.8 %blend.1 = (bf16[128,8,128]{2,1,0:T(8,128)(2,1)}, bf16[12,1024,128]{2,1,0:T(8,128)(2,1)}) custom-call(s32[128]{0:T(128)} %order_hbm.3, s32[128]{0:T(128)} %length_hbm.3, f32[1,768]{1,0:T(1,128)} %amp_hbm.1, s32[1,128]{1,0:T(1,128)} %bitcast.1, bf16[1,1,64,3072]{3,2,1,0:T(8,128)(2,1)} %control_hbm.1, bf16[1,64,64]{2,1,0:T(8,128)(2,1)} %vertical_hbm.1, ...), custom_call_target="tpu_custom_call" | custom-call | tf_op jit(solution)/shard_map/blend/pallas_call | solution.py:538
  43.8 3.5 %synthesis.1 = bf16[1,1,64,3072]{3,2,1,0:T(8,128)(2,1)} custom-call(s32[128]{0:T(128)} %order_hbm.3, s32[128]{0:T(128)} %length_hbm.3, bf16[128,8,128]{2,1,0:T(8,128)(2,1)} %get-tuple-element.7.balanced_hbm, bf16[12,1024,128]{2,1,0:T(8,128)(2,1)} %get-tuple-element.8.table_hbm), custom_call_target="tpu_custom_call" | custom-call | tf_op jit(solution)/shard_map/synthesis/pallas_call | solution.py:578

commit v5 on v4

--- a/solution.py
+++ b/solution.py
@@ -22,6 +22,10 @@
 
 def nt_dot(a, b):
     return lax.dot_general(a, b, (((1,), (1,)), ((), ())), preferred_element_type=F32)
+
+
+def row_of(lat_total):
+    return ROW if lat_total % ROW == 0 else 2
 
 
 def own_length(order_ref, length_ref):
@@ -294,7 +298,7 @@
     me = lax.axis_index("lat")
     var = lax.axis_index("var")
     var_total = lax.axis_size("var")
-    row_size = ROW if lat_total % ROW == 0 else 2
+    row_size = row_of(lat_total)
     columns = lat_total // row_size
     chips = row_size // 2
     core, spot, line = me % 2, me // 2 % chips, me // row_size
@@ -317,15 +321,15 @@
     def greet(sem, **where):
         pl.semaphore_signal(sem, 1, device_id=where, device_id_type=MESH)
 
-    def greet_column(sem_of):
+    def greet_column(sem):
         for step in range(1, columns):
-            greet(sem_of(step), lat=(line + step) % columns * row_size + me % row_size)
+            greet(sem, lat=(line + step) % columns * row_size + me % row_size)
 
     arriving[0].start()
     arriving[1].start()
     for step in range(1, row_size):
         greet(barrier, lat=line * row_size + (me + step) % row_size)
-    greet_column(lambda step: barrier)
+    greet_column(barrier)
     for step in range(1, var_total):
         greet(barrier, var=(var + step) % var_total)
     for copy in arriving[2:]:
@@ -339,10 +343,11 @@
     table_copy = pltpu.make_async_copy(table_ref, table_hbm, table_sem)
     table_copy.start()
     pl.semaphore_wait(barrier, row_size - 1 + columns - 1 + var_total - 1)
-    greet_column(lambda step: line_sem.at[columns - step])
+    greet_column(line_sem)
     arriving[2].wait()
     arriving[3].wait()
     analyse(length, per_peer, control_ref, vertical_ref, coeff_ref, table_ref, level_ref)
+    pl.semaphore_wait(line_sem, columns - 1)
 
     def to_peer(src_ref, dst_ref, peer, src_sem, dst_sem):
         return pltpu.make_async_remote_copy(
@@ -369,19 +374,17 @@
 
         lax.fori_loop(1 if own else 0, row_size, one, 0, unroll=True)
 
-    def first(distance):
-        pl.semaphore_wait(line_sem.at[distance], 1)
-        there = (line + distance) % columns
-        to_line(there, coeff_ref, recv_ref, send_sem, recv_sem, own=False)
+    def first(there, own=False):
+        to_line(there, coeff_ref, recv_ref, send_sem, recv_sem, own)
 
     def send(step, carry):
-        first(columns // 2 + step)
-        first(columns // 2 - step)
+        first((line + columns // 2 + step) % columns)
+        first((line + columns // 2 - step) % columns)
         return carry
 
-    to_line(line, coeff_ref, recv_ref, send_sem, recv_sem, own=True)
-    first(columns // 2)
+    first((line + columns // 2) % columns)
     lax.fori_loop(1, columns // 2, send, 0)
+    first(line, own=True)
     own = pltpu.make_async_copy(coeff_ref.at[me], recv_ref.at[me], local_sem)
     own.start()
     for copy in arriving[4:]:
@@ -445,21 +448,21 @@
         _, here = piece_rows(piece)
         pltpu.make_async_copy(root_ref.at[here], root_ref.at[here], root_recv_sem.at[piece]).wait()
 
+    def relay(step):
+        piece = jnp.where(var == 1, step, columns - 1 - step)
+        await_root(piece)
+        root_copy(piece, 2).start()
+
+    between = (var == 1) | (var == 3)
     if relayed:
-        @pl.when((var == 1) | (var == 3))
-        def _():
-            def relay(step, carry):
-                piece = jnp.where(var == 1, step, columns - 1 - step)
-                await_root(piece)
-                root_copy(piece, 2).start()
-                return carry
-
-            lax.fori_loop(0, half, relay, 0)
+        pl.when(between)(lambda: relay(0))
 
     def one_piece(step, carry):
         outside_in = jnp.where(step % 2 == 0, step // 2, columns - 1 - step // 2)
         piece = jnp.where(var == 1, step, jnp.where(var == 3, columns - 1 - step, outside_in))
         there, here = piece_rows(piece)
+        if relayed:
+            pl.when(between & (step + 1 < half))(lambda: relay(step + 1))
 
         waiting = var > 0
         if relayed:
@@ -502,7 +505,7 @@
 
     if relayed:
 
-        @pl.when((var == 1) | (var == 3))
+        @pl.when(between)
         def _():
             sent_roots(half)
 
@@ -518,6 +521,7 @@
     groups = lat_total // 4
     quarter = lons // 4
     blocks = quarter // LANES
+    columns = lat_total // row_of(lat_total)
     anywhere = pl.BlockSpec(memory_space=pl.ANY)
     seeds = pltpu.VMEM((groups + 4 * SUBS, quarter), F32)
     packed = jax.ShapeDtypeStruct((lat_total, SUBS, LANES), BF16)
@@ -554,13 +558,13 @@
             pltpu.VMEM((lat_total, per_peer * LANES), F32),
             pltpu.VMEM((lat_total, per_peer * LANES), BF16),
             block,
-            pltpu.SemaphoreType.REGULAR((lat_total,)),
+            pltpu.SemaphoreType.REGULAR,
             dma(()),
             dma(()),
             dma(()),
             dma(()),
             dma(()),
-            dma((lat_total,)),
+            dma((columns,)),
             dma(()),
             dma(()),
         ],

time: 47.7 us -> 45.2 us (0.948)
  the two profiles are of different devices: /device:TPU:7 before, /device:TPU:5 now
where the time goes in v5:
time: 45.2 us; the launch traced here: 45 us
  Pallas kernels  45 us (100%)
    pallas_call x1, Pallas kernels, body(): pl.pallas_call(functools.partial(blend_kernel, per_peer), name='blend', o...  41.6 us
    pallas_call x1, Pallas kernels, body(): pl.pallas_call(functools.partial(synthesis_kernel, per_peer), name='synth...  3.46 us

profile of v5, /device:TPU:5, one launch (start us, length us, event | category | flops | bytes accessed | tf_op | source)
XLA Modules:
  0.0 45.0 jit_solution(5954871615868774821)
XLA Ops:
  0.0 41.6 %blend.1 = (bf16[128,8,128]{2,1,0:T(8,128)(2,1)}, bf16[12,1024,128]{2,1,0:T(8,128)(2,1)}) custom-call(s32[128]{0:T(128)} %order_hbm.3, s32[128]{0:T(128)} %length_hbm.3, f32[1,768]{1,0:T(1,128)} %amp_hbm.1, s32[1,128]{1,0:T(1,128)} %bitcast.1, bf16[1,1,64,3072]{3,2,1,0:T(8,128)(2,1)} %control_hbm.1, bf16[1,64,64]{2,1,0:T(8,128)(2,1)} %vertical_hbm.1, ...), custom_call_target="tpu_custom_call" | custom-call | tf_op jit(solution)/shard_map/blend/pallas_call | solution.py:542
  41.6 3.5 %synthesis.1 = bf16[1,1,64,3072]{3,2,1,0:T(8,128)(2,1)} custom-call(s32[128]{0:T(128)} %order_hbm.3, s32[128]{0:T(128)} %length_hbm.3, bf16[128,8,128]{2,1,0:T(8,128)(2,1)} %get-tuple-element.7.balanced_hbm, bf16[12,1024,128]{2,1,0:T(8,128)(2,1)} %get-tuple-element.8.table_hbm), custom_call_target="tpu_custom_call" | custom-call | tf_op jit(solution)/shard_map/synthesis/pallas_call | solution.py:582

commit v6 on v5

--- a/solution.py
+++ b/solution.py
@@ -24,8 +24,22 @@
     return lax.dot_general(a, b, (((1,), (1,)), ((), ())), preferred_element_type=F32)
 
 
+def write_packed(ref, here, rows):
+    for j in range(ref.shape[-1] // LANES):
+        ref[here, :, pl.ds(j * LANES, LANES)] = rows[:, 2 * j : 2 * j + 2, :].astype(BF16)
+
+
+def read_packed(ref, target_ref):
+    for j in range(ref.shape[-1] // LANES):
+        target_ref[:, pl.ds(2 * j, 2), :] = ref[:, :, pl.ds(j * LANES, LANES)].astype(F32)
+
+
 def row_of(lat_total):
     return ROW if lat_total % ROW == 0 else 2
+
+
+def far_first(count):
+    return sorted(range(1, count), key=lambda step: -min(step, count - step))
 
 
 def own_length(order_ref, length_ref):
@@ -151,7 +165,7 @@
         )
         part = nt_dot(table_rows(table_ref, rem, rows, 0, 2 * blocks), mixed)
         part = part.reshape(groups, SUBS, LANES) * scale[rem * groups : (rem + 1) * groups]
-        coeff_ref[pl.ds(rem * groups, groups)] = part.astype(BF16)
+        write_packed(coeff_ref, pl.ds(rem * groups, groups), part)
 
 
 def synthesis_kernel(
@@ -164,6 +178,7 @@
     order_ref,
     length_ref,
     balanced_ref,
+    spec_ref,
     out_ref,
     table_ref,
     wide_ref,
@@ -196,9 +211,8 @@
     length = own_length(order_ref, length_ref)
     arriving[2].wait()
     wave, held = row_wave(lat_total, per_peer)
-    spectra = jnp.where(
-        held & (wave <= (length - 1) // 2), balanced_ref[...].astype(F32), 0.0
-    )
+    read_packed(balanced_ref, spec_ref)
+    spectra = jnp.where(held & (wave <= (length - 1) // 2), spec_ref[...], 0.0)
     turned = spectra.reshape(lat_total * SUBS, LANES).T.astype(BF16)
 
     def parts(rem):
@@ -300,8 +314,7 @@
     var_total = lax.axis_size("var")
     row_size = row_of(lat_total)
     columns = lat_total // row_size
-    chips = row_size // 2
-    core, spot, line = me % 2, me // 2 % chips, me // row_size
+    line, place = lax.div(me, row_size), lax.rem(me, row_size)
     barrier = pltpu.get_barrier_semaphore()
     arriving = []
     for index, (source, target) in enumerate(
@@ -322,16 +335,16 @@
         pl.semaphore_signal(sem, 1, device_id=where, device_id_type=MESH)
 
     def greet_column(sem):
-        for step in range(1, columns):
-            greet(sem, lat=(line + step) % columns * row_size + me % row_size)
+        for step in far_first(columns):
+            greet(sem, lat=lax.rem(line + step, columns) * row_size + place)
 
     arriving[0].start()
     arriving[1].start()
-    for step in range(1, row_size):
-        greet(barrier, lat=line * row_size + (me + step) % row_size)
+    for step in far_first(row_size):
+        greet(barrier, lat=line * row_size + lax.rem(place + step, row_size))
     greet_column(barrier)
     for step in range(1, var_total):
-        greet(barrier, var=(var + step) % var_total)
+        greet(barrier, var=lax.rem(var + step, var_total))
     for copy in arriving[2:]:
         copy.start()
 
@@ -361,7 +374,7 @@
 
     def to_line(there, src_ref, dst_ref, src_sem, dst_sem, own=None):
         def one(offset, carry):
-            peer = there * row_size + (me + offset) % row_size
+            peer = there * row_size + lax.rem(place + offset, row_size)
 
             def start():
                 to_peer(src_ref, dst_ref, peer, src_sem, dst_sem).start()
@@ -378,11 +391,11 @@
         to_line(there, coeff_ref, recv_ref, send_sem, recv_sem, own)
 
     def send(step, carry):
-        first((line + columns // 2 + step) % columns)
-        first((line + columns // 2 - step) % columns)
+        first(lax.rem(line + columns // 2 + step, columns))
+        first(lax.rem(line + columns // 2 - step, columns))
         return carry
 
-    first((line + columns // 2) % columns)
+    first(lax.rem(line + columns // 2, columns))
     lax.fori_loop(1, columns // 2, send, 0)
     first(line, own=True)
     own = pltpu.make_async_copy(coeff_ref.at[me], recv_ref.at[me], local_sem)
@@ -406,7 +419,7 @@
         pltpu.make_async_copy(ref.at[rest], ref.at[rest], sem).wait()
 
     settle(recv_ref, recv_sem)
-    wide_ref[...] = recv_ref[...].astype(F32)
+    read_packed(recv_ref, wide_ref)
     received = [wide_ref[:, sub, :].astype(BF16) for sub in range(per_peer)]
     product = jnp.dot(slot_mat, jnp.concatenate(received, axis=1), preferred_element_type=F32)
     scaled = []
@@ -416,7 +429,7 @@
     product_ref[...] = jnp.concatenate(scaled, axis=1)
 
     def piece_rows(piece):
-        there = (line + columns // 2 + piece) % columns
+        there = lax.rem(line + columns // 2 + piece, columns)
         return there, pl.ds(pl.multiple_of(there * row_size, row_size), row_size)
 
     def root_copy(piece, target):
@@ -482,7 +495,7 @@
             blended = product_ref[here, pl.ds(sub * LANES, LANES)]
             addend = lifted[sub * row_size : (sub + 1) * row_size]
             wide_ref[here, sub, :] = blended + jnp.where(var > 0, addend, 0.0)
-        mixed_ref[here] = wide_ref[here].astype(BF16)
+        write_packed(mixed_ref, here, wide_ref[here])
 
         to_line(there, mixed_ref, balanced_hbm, back_send_sem, back_recv_sem)
         return carry
@@ -524,7 +537,7 @@
     columns = lat_total // row_of(lat_total)
     anywhere = pl.BlockSpec(memory_space=pl.ANY)
     seeds = pltpu.VMEM((groups + 4 * SUBS, quarter), F32)
-    packed = jax.ShapeDtypeStruct((lat_total, SUBS, LANES), BF16)
+    packed = jax.ShapeDtypeStruct((lat_total, 2, per_peer // 2 * LANES), BF16)
     table = jax.ShapeDtypeStruct((2 * blocks, lat_total * SUBS, LANES), BF16)
     table_vmem = pltpu.VMEM(table.shape, BF16)
     block = pltpu.VMEM(packed.shape, BF16)
@@ -554,7 +567,7 @@
             pltpu.VMEM((levels, lons + LANES), BF16),
             block,
             block,
-            pltpu.VMEM(packed.shape, F32),
+            pltpu.VMEM((lat_total, SUBS, LANES), F32),
             pltpu.VMEM((lat_total, per_peer * LANES), F32),
             pltpu.VMEM((lat_total, per_peer * LANES), BF16),
             block,
@@ -589,6 +602,7 @@
             inputs[0],
             inputs[1],
             block,
+            pltpu.VMEM((lat_total, SUBS, LANES), F32),
             pltpu.VMEM((levels, lons), BF16),
             table_vmem,
             pltpu.VMEM((levels, lons + LANES), F32),

time: 45.2 us -> 42.6 us (0.942)
  the two profiles are of different devices: /device:TPU:5 before, /device:TPU:7 now
where the time goes in v6:
time: 42.6 us; the launch traced here: 41.8 us
  Pallas kernels  41.8 us (98%)
    pallas_call x1, Pallas kernels, body(): pl.pallas_call(functools.partial(blend_kernel, per_peer), name='blend', o...  38.3 us
    pallas_call x1, Pallas kernels, body(): pl.pallas_call(functools.partial(synthesis_kernel, per_peer), name='synth...  3.49 us

profile of v6, /device:TPU:7, one launch (start us, length us, event | category | flops | bytes accessed | tf_op | source)
XLA Modules:
  0.0 41.8 jit_solution(2114204172156275947)
XLA Ops:
  0.0 38.3 %blend.1 = (bf16[128,2,384]{2,1,0:T(2,128)(2,1)}, bf16[12,1024,128]{2,1,0:T(8,128)(2,1)}) custom-call(s32[128]{0:T(128)} %order_hbm.3, s32[128]{0:T(128)} %length_hbm.3, f32[1,768]{1,0:T(1,128)} %amp_hbm.1, s32[1,128]{1,0:T(1,128)} %bitcast.1, bf16[1,1,64,3072]{3,2,1,0:T(8,128)(2,1)} %control_hbm.1, bf16[1,64,64]{2,1,0:T(8,128)(2,1)} %vertical_hbm.1, ...), custom_call_target="tpu_custom_call" | custom-call | tf_op jit(solution)/shard_map/blend/pallas_call | solution.py:555
  38.3 3.5 %synthesis.1 = bf16[1,1,64,3072]{3,2,1,0:T(8,128)(2,1)} custom-call(s32[128]{0:T(128)} %order_hbm.3, s32[128]{0:T(128)} %length_hbm.3, bf16[128,2,384]{2,1,0:T(2,128)(2,1)} %get-tuple-element.7.balanced_hbm, bf16[12,1024,128]{2,1,0:T(8,128)(2,1)} %get-tuple-element.8.table_hbm), custom_call_target="tpu_custom_call" | custom-call | tf_op jit(solution)/shard_map/synthesis/pallas_call | solution.py:595

commit v7 on v6

--- a/solution.py
+++ b/solution.py
@@ -468,14 +468,18 @@
 
     between = (var == 1) | (var == 3)
     if relayed:
-        pl.when(between)(lambda: relay(0))
+        @pl.when(between)
+        def _():
+            relay(0)
+            relay(1)
+
 
     def one_piece(step, carry):
         outside_in = jnp.where(step % 2 == 0, step // 2, columns - 1 - step // 2)
         piece = jnp.where(var == 1, step, jnp.where(var == 3, columns - 1 - step, outside_in))
         there, here = piece_rows(piece)
         if relayed:
-            pl.when(between & (step + 1 < half))(lambda: relay(step + 1))
+            pl.when(between & (step + 2 < half))(lambda: relay(step + 2))
 
         waiting = var > 0
         if relayed:

time: 42.6 us -> 42.8 us (level)
  no operation moved by 1% of the time
where the time goes in v7:
time: 42.8 us; the launch traced here: 42.2 us
  Pallas kernels  42.2 us (99%)
    pallas_call x1, Pallas kernels, body(): pl.pallas_call(functools.partial(blend_kernel, per_peer), name='blend', o...  38.7 us
    pallas_call x1, Pallas kernels, body(): pl.pallas_call(functools.partial(synthesis_kernel, per_peer), name='synth...  3.49 us

profile of v7, /device:TPU:7, one launch (start us, length us, event | category | flops | bytes accessed | tf_op | source)
XLA Modules:
  0.0 42.2 jit_solution(7446713729591897937)
XLA Ops:
  0.0 38.7 %blend.1 = (bf16[128,2,384]{2,1,0:T(2,128)(2,1)}, bf16[12,1024,128]{2,1,0:T(8,128)(2,1)}) custom-call(s32[128]{0:T(128)} %order_hbm.3, s32[128]{0:T(128)} %length_hbm.3, f32[1,768]{1,0:T(1,128)} %amp_hbm.1, s32[1,128]{1,0:T(1,128)} %bitcast.1, bf16[1,1,64,3072]{3,2,1,0:T(8,128)(2,1)} %control_hbm.1, bf16[1,64,64]{2,1,0:T(8,128)(2,1)} %vertical_hbm.1, ...), custom_call_target="tpu_custom_call" | custom-call | tf_op jit(solution)/shard_map/blend/pallas_call | solution.py:559
  38.7 3.5 %synthesis.1 = bf16[1,1,64,3072]{3,2,1,0:T(8,128)(2,1)} custom-call(s32[128]{0:T(128)} %order_hbm.3, s32[128]{0:T(128)} %length_hbm.3, bf16[128,2,384]{2,1,0:T(2,128)(2,1)} %get-tuple-element.7.balanced_hbm, bf16[12,1024,128]{2,1,0:T(8,128)(2,1)} %get-tuple-element.8.table_hbm), custom_call_target="tpu_custom_call" | custom-call | tf_op jit(solution)/shard_map/synthesis/pallas_call | solution.py:599
